TPU v7x, 1024 devices: a whole 4x8x16 slice. The times are simulated.
1024 devices in a mesh: tile: 64 (over z, x_hi, core), mem: 16 (over x_lo, y).
Axes of the slice: x: 4 (x_hi: 2, x_lo: 2; x = x_hi * 2 + x_lo), y: 8, z: 16, core: 2. Of those that a mesh axis runs over, the one named last changes fastest.
Arguments:
- right_side: float32 [64, 256, 16, 256], P('tile', 'mem'), may hold values from -6 to 6
- perturbations: bfloat16 [64, 256, 6, 16, 256], P('tile', 'mem'), may hold values from -0.375 to 0.375
- precision: float32 [64, 6, 16, 256], P('tile'), may hold values from 5 to 40
- covered: int32 [64, 2, 16], P('tile'), may hold values 0 or 1
Outputs:
- weights: float32 [64, 256, 16, 256], P('tile', 'mem')
- residual: float32 [64, 256, 16, 256], P('tile', 'mem')
All inputs are finite; a program needn't handle non-finite values. No bound on the sum of `covered` on one device may be relied on, other than what follows from the above.
Results may differ from a plain program's by a relative error of at most 0.006.
Values sent between devices are 32-bit elements; how exact they have to be, the bound alone decides.
A program may use at most 32 MiB of HBM per device.

v0:
```python
import jax
import jax.numpy as jnp
from jax import lax
from jax.sharding import Mesh
from jax.sharding import PartitionSpec as P

ITERS = 2
TILE = ("tile_0", "tile_1", "tile_2")
MEM = ("mem_0", "mem_1")
TILE_MEM = ("tile_0", "tile_1", "tile_2", "mem_0", "mem_1")


def passed_along(value, axis, steps):
    count = lax.axis_size(axis)
    first, last = (max(0, -steps), min(count, count - steps))
    return lax.ppermute(value, axis, [(source, source + steps) for source in range(first, last)])


def padded_2(cells, sides, width):
    for axis, dim in sides:
        count = lax.axis_size(axis)
        head = lax.slice_in_dim(cells, 0, width, axis=dim)
        tail = lax.slice_in_dim(cells, cells.shape[dim] - width, cells.shape[dim], axis=dim)
        cells = jnp.concatenate(
            [
                lax.ppermute(tail, axis, [(i, (i + 1) % count) for i in range(count)]),
                cells,
                lax.ppermute(head, axis, [((i + 1) % count, i) for i in range(count)]),
            ],
            axis=dim,
        )
    return cells


def in_blocks(value, dim, devices):
    before, after = (value.shape[:dim], value.shape[dim + 1 :])
    return jnp.moveaxis(value.reshape(*before, devices, -1, *after), dim, 0)


def sent_and_summed(value, axis, dim):
    devices = lax.axis_size(axis)
    pieces = lax.all_to_all(in_blocks(value, dim, devices), axis, 0, 0, tiled=True)
    return jnp.sum(pieces, axis=0)


def joined_along(pieces, dim):
    pieces = jnp.moveaxis(pieces, 0, dim)
    lengths = pieces.shape
    return pieces.reshape(*lengths[:dim], lengths[dim] * lengths[dim + 1], *lengths[dim + 2 :])


def sent_to_all(value, axis):
    copies = jnp.broadcast_to(value, (lax.axis_size(axis), *value.shape))
    return lax.all_to_all(copies, axis, split_axis=0, concat_axis=0, tiled=True)


def gather_directly(value, axis, dim):
    return joined_along(sent_to_all(value, axis), dim)


def by_axis(value, axes):
    for axis in axes:
        value = lax.psum(value, axis)
    return value


def filter_taps():
    offsets = jnp.arange(-8, 9).astype(jnp.float32)
    raw = jnp.exp(-offsets * offsets / 32.0)
    return raw / jnp.sqrt(jnp.sum(jnp.exp(-offsets * offsets / 16.0)))


def smooth(field):
    taps = filter_taps()
    height = field.shape[1]
    width = field.shape[2]
    above = passed_along(field[:, height - 8 :, :], TILE, 8)
    below = passed_along(field[:, :8, :], TILE, -8)
    padded = jnp.concatenate([above, field, below], axis=1)
    along = jnp.zeros_like(field)
    for j in range(17):
        along = along + taps[j] * padded[:, j : j + height, :]
    sided = padded_2(along, ((TILE, 2),), 8)
    result = jnp.zeros_like(field)
    for j in range(17):
        result = result + taps[j] * sided[:, :, j : j + width]
    return result


def apply_operator(direction, members_data, obs_weight):
    smoothed = smooth(direction)
    partial_terms = jnp.einsum("kvyx,kyx->vyx", members_data.astype(jnp.float32), smoothed)
    share = sent_and_summed(partial_terms, MEM, 1)
    rows = share.shape[1]
    local_weight = lax.dynamic_slice_in_dim(obs_weight, lax.axis_index(MEM) * rows, rows, 1)
    weighted = gather_directly(local_weight * share, MEM, 1)
    back = jnp.einsum("kvyx,vyx->kyx", members_data.astype(jnp.float32), weighted)
    return direction + smooth(back)


def two_products(residual, image):
    return (
        by_axis(jnp.sum(residual * residual), TILE_MEM),
        by_axis(jnp.sum(residual * image), TILE_MEM),
    )


def local(right_side, perturbations, precision, covered):
    members_data = perturbations[0]
    mask = covered[0].astype(jnp.float32)
    levels = precision.shape[1]
    height = precision.shape[2]
    width = precision.shape[3]
    obs_weight = (
        precision[0].reshape(levels, height // 8, 8, width // 16, 16) * mask[None, :, None, :, None]
    ).reshape(levels, height, width)
    source = right_side[0]
    weights = jnp.zeros_like(source)
    residual = source
    image = apply_operator(residual, members_data, obs_weight)
    norm_now, product = two_products(residual, image)
    length = norm_now / product
    direction, along = (residual, image)
    for step in range(ITERS):
        weights = weights + length * direction
        residual = residual - length * along
        if step + 1 < ITERS:
            image = apply_operator(residual, members_data, obs_weight)
            norm_next, product = two_products(residual, image)
            ratio = norm_next / norm_now
            length = norm_next / (product - ratio * norm_next / length)
            direction = residual + ratio * direction
            along = image + ratio * along
            norm_now = norm_next
    return (weights[None], residual[None])


def solution(mesh):
    finer = Mesh(
        mesh.devices.reshape(16, 2, 2, 2, 8), ("tile_0", "tile_1", "tile_2", "mem_0", "mem_1")
    )
    in_specs = (
        P(TILE, MEM, None, None),
        P(TILE, MEM, None, None, None),
        P(TILE, None, None, None),
        P(TILE, None, None),
    )
    out_specs = (P(TILE, MEM, None, None), P(TILE, MEM, None, None))
    return jax.shard_map(local, mesh=finer, in_specs=in_specs, out_specs=out_specs, check_vma=False)
```

profile of v0, /device:TPU:64, one launch (start us, length us, event | category | flops | bytes accessed | tf_op | source)
XLA Modules:
  0.0 390.4 jit_solution(15509579184658797857)
XLA Ops:
  0.6 1.0 fusion.385
  1.7 6.1 %collective-permute-start = (f32[16,8,256]{2,1,0:T(8,128)S(1)}, f32[16,8,256]{2,1,0:T(8,128)S(1)}, u32[]{:S(2)}, u32[]{:S(2)}) collective-permute-start(f32[16,8,256]{2,1,0:T(8,128)S(1)} %get-tuple-element.44), channel_id=1, source_target_pairs={{0,128},{16,144},{32,160},{48,176},{64,192},{80,208},{96,224},{112... | collective-permute-start | bytes 393224 | tf_op jit(solution)/shard_map/ppermute | solution.py:16
  7.8 1.3 collective-permute-start.1
  9.1 0.6 exponential_reduce_fusion
  10.4 0.7 fusion.386
  11.1 9.1 %collective-permute-done.1 = f32[16,8,256]{2,1,0:T(8,128)S(1)} collective-permute-done((f32[16,8,256]{2,1,0:T(8,128)S(1)}, f32[16,8,256]{2,1,0:T(8,128)S(1)}, u32[]{:S(2)}, u32[]{:S(2)}) %collective-permute-start.1) | collective-permute-done | bytes 131104 | tf_op jit(solution)/shard_map/ppermute | solution.py:16
  20.2 11.2 %fusion.319 = f32[16,16,256]{2,1,0:T(8,128)S(1)} fusion(f32[16,16,256]{2,1,0:T(8,128)S(1)} %bitcast.89, f32[16,8,256]{2,1,0:T(8,128)S(1)} %collective-permute-done.1, f32[16,8,256]{2,1,0:T(8,128)S(1)} %collective-permute-done, f32[]{:T(128)} %bitcast.27, f32[]{:T(128)} %bitcast.26, f32[]{:T(128)} %bitcast.25, f32[]{:T(128)} %bitcast.24, f32[]{:T(128)} %bitcast.23, ...), kind=kLoop, calls=%fused_computation.547 | loop fusion | flops 3211264 | bytes 786500 | tf_op jit(solution)/shard_map/add | solution.py:82
  31.5 2.1 collective-permute-start.2
  33.6 6.0 %collective-permute-start.3 = (f32[16,16,8]{2,1,0:T(8,128)S(1)}, f32[16,16,8]{2,1,0:T(8,128)S(1)}, u32[]{:S(2)}, u32[]{:S(2)}) collective-permute-start(f32[16,16,8]{2,1,0:T(8,128)S(1)} %get-tuple-element.43), channel_id=1, source_target_pairs={{16,0},{32,16},{48,32},{64,48},{80,64},{96,80},{112,96},{128,112},... | collective-permute-start | bytes 24584 | tf_op jit(solution)/shard_map/ppermute | solution.py:28
  39.6 0.7 collective-permute-done.2
  40.3 1.8 collective-permute-done.3
  42.1 12.1 %fusion.275 = f32[16,256,16]{1,0,2:T(8,128)S(1)} fusion(f32[16,16,256]{2,1,0:T(8,128)S(1)} %fusion.319, f32[16,16,8]{2,1,0:T(8,128)S(1)} %collective-permute-done.3, f32[16,16,8]{2,1,0:T(8,128)S(1)} %collective-permute-done.2, f32[]{:T(128)} %bitcast.27, f32[]{:T(128)} %bitcast.26, f32[]{:T(128)} %bitcast.25, f32[]{:T(128)} %bitcast.24, f32[]{:T(128)} %bitcast.23, ...), kind=kLoop, calls=%fused_computation.503 | loop fusion | flops 3211264 | bytes 540740
  54.3 0.2 fusion
  54.5 0.7 copy.12
  55.2 8.2 %all-to-all-start = ((f32[16,6,1,256]{3,2,1,0:T(1,128)}), f32[16,6,1,256]{3,2,1,0:T(1,128)S(1)}, u32[]{:S(2)}, u32[]{:S(2)}) async-start(f32[16,6,1,256]{3,2,1,0:T(1,128)} %copy.12), calls=%async_computation | async-start | bytes 196608 | tf_op jit(solution)/shard_map/all_to_all | solution.py:42
  63.6 8.3 %all-to-all-done = f32[16,6,1,256]{3,2,1,0:T(1,128)S(1)} async-done(((f32[16,6,1,256]{3,2,1,0:T(1,128)}), f32[16,6,1,256]{3,2,1,0:T(1,128)S(1)}, u32[]{:S(2)}, u32[]{:S(2)}) %all-to-all-start) | async-done | bytes 98336 | tf_op jit(solution)/shard_map/all_to_all | solution.py:42
  72.0 0.8 reshape_multiply_fusion.1
  72.9 12.3 %all_to_all.20 = f32[16,6,1,256]{3,2,1,0:T(1,128)S(1)} all-to-all(f32[16,6,1,256]{3,2,1,0:T(1,128)S(1)} %broadcast_in_dim.13), channel_id=1, replica_groups=mesh['tile_0'=16,'tile_1'=2,'tile_2'=2,'mem_0'=2,'mem_1'=8] {'mem_0','me..., dimensions={0} | all-to-all | bytes 196608 | tf_op jit(solution)/shard_map/all_to_all | solution.py:54
  85.2 0.2 fusion.2
  85.4 4.2 %collective-permute-start.4 = (f32[16,8,256]{2,1,0:T(8,128)S(1)}, f32[16,8,256]{2,1,0:T(8,128)S(1)}, u32[]{:S(2)}, u32[]{:S(2)}) collective-permute-start(f32[16,8,256]{2,1,0:T(8,128)S(1)} %get-tuple-element.40), channel_id=1, source_target_pairs={{0,128},{16,144},{32,160},{48,176},{64,192},{80,208},{96,224},{112... | collective-permute-start | bytes 393224 | tf_op jit(solution)/shard_map/ppermute | solution.py:16
  89.6 1.3 collective-permute-start.5
  90.9 3.5 collective-permute-done.4
  94.4 7.5 %collective-permute-done.5 = f32[16,8,256]{2,1,0:T(8,128)S(1)} collective-permute-done((f32[16,8,256]{2,1,0:T(8,128)S(1)}, f32[16,8,256]{2,1,0:T(8,128)S(1)}, u32[]{:S(2)}, u32[]{:S(2)}) %collective-permute-start.5) | collective-permute-done | bytes 131104 | tf_op jit(solution)/shard_map/ppermute | solution.py:16
  101.9 11.2 %fusion.230 = f32[16,16,256]{2,1,0:T(8,128)S(1)} fusion(f32[16,16,256]{2,1,0:T(8,128)S(1)} %bitcast.91, f32[16,8,256]{2,1,0:T(8,128)S(1)} %collective-permute-done.5, f32[16,8,256]{2,1,0:T(8,128)S(1)} %collective-permute-done.4, f32[]{:T(128)} %bitcast.27, f32[]{:T(128)} %bitcast.26, f32[]{:T(128)} %bitcast.25, f32[]{:T(128)} %bitcast.24, f32[]{:T(128)} %bitcast.23, ...), kind=kLoop, calls=%fused_computation.458 | loop fusion | flops 3211264 | bytes 786500 | tf_op jit(solution)/shard_map/add | solution.py:82
  113.2 1.9 collective-permute-start.6
  115.1 6.0 %collective-permute-start.7 = (f32[16,16,8]{2,1,0:T(8,128)S(1)}, f32[16,16,8]{2,1,0:T(8,128)S(1)}, u32[]{:S(2)}, u32[]{:S(2)}) collective-permute-start(f32[16,16,8]{2,1,0:T(8,128)S(1)} %get-tuple-element.39), channel_id=1, source_target_pairs={{16,0},{32,16},{48,32},{64,48},{80,64},{96,80},{112,96},{128,112},... | collective-permute-start | bytes 24584 | tf_op jit(solution)/shard_map/ppermute | solution.py:28
  121.2 0.7 collective-permute-done.6
  121.9 1.8 collective-permute-done.7
  123.7 12.8 %multiply_reduce_fusion.2 = (f32[]{:T(128)}, f32[]{:T(128)}, f32[16,16,256]{2,1,0:T(8,128)S(1)}) fusion(f32[1,16,16,256]{3,2,1,0:T(8,128)S(1)} %copy-done.1, f32[16,16,8]{2,1,0:T(8,128)S(1)} %collective-permute-done.7, f32[16,16,256]{2,1,0:T(8,128)S(1)} %fusion.230, f32[]{:T(128)} %bitcast.27, f32[]{:T(128)} %bitcast.26, f32[]{:T(128)} %bitcast.25, ...), kind=kLoop, calls=%fused_computation.625 | loop fusion | flops 3538942 | bytes 802892 | tf_op jit(solution)/shard_map/reduce_sum | solution.py:104
  136.4 31.9 %all-reduce.1 = (f32[]{:T(128)}, f32[]{:T(128)}) all-reduce(f32[]{:T(128)} %get-tuple-element.5, f32[]{:T(128)} %get-tuple-element.4), channel_id=1, replica_groups=mesh['tile_0'=16,'tile_1'=2,'tile_2'=2,'mem_0'=2,'mem_1'=8] {'tile_0'}, use_global_device_ids=true, to_apply=%region_1.0 | all-reduce | flops 2 | bytes 16 | tf_op jit(solution)/shard_map/psum | solution.py:63
  168.4 7.1 %all-reduce.9 = (f32[]{:T(128)}, f32[]{:T(128)}) all-reduce(f32[]{:T(128)} %get-tuple-element.8, f32[]{:T(128)} %get-tuple-element.9), channel_id=1, replica_groups=mesh['tile_0'=16,'tile_1'=2,'tile_2'=2,'mem_0'=2,'mem_1'=8] {'tile_1'}, use_global_device_ids=true, to_apply=%region_2.0 | all-reduce | flops 2 | bytes 16 | tf_op jit(solution)/shard_map/psum | solution.py:63
  175.4 3.2 all-reduce.7
  178.6 5.6 %all-reduce.5 = (f32[]{:T(128)}, f32[]{:T(128)}) all-reduce(f32[]{:T(128)} %get-tuple-element.20, f32[]{:T(128)} %get-tuple-element.21), channel_id=1, replica_groups=mesh['tile_0'=16,'tile_1'=2,'tile_2'=2,'mem_0'=2,'mem_1'=8] {'mem_0'}, use_global_device_ids=true, to_apply=%region_4.0 | all-reduce | flops 2 | bytes 16 | tf_op jit(solution)/shard_map/psum | solution.py:63
  184.2 16.2 %all-reduce.3 = (f32[]{:T(128)}, f32[]{:T(128)}) all-reduce(f32[]{:T(128)} %get-tuple-element.16, f32[]{:T(128)} %get-tuple-element.17), channel_id=1, replica_groups=mesh['tile_0'=16,'tile_1'=2,'tile_2'=2,'mem_0'=2,'mem_1'=8] {'mem_1'}, use_global_device_ids=true, to_apply=%region_5.0 | all-reduce | flops 2 | bytes 16 | tf_op jit(solution)/shard_map/psum | solution.py:63
  201.8 3.7 collective-permute-start.8
  205.6 1.3 collective-permute-start.9
  206.9 2.3 collective-permute-done.8
  209.1 4.5 %collective-permute-done.9 = f32[16,8,256]{2,1,0:T(8,128)S(1)} collective-permute-done((f32[16,8,256]{2,1,0:T(8,128)S(1)}, f32[16,8,256]{2,1,0:T(8,128)S(1)}, u32[]{:S(2)}, u32[]{:S(2)}) %collective-permute-start.9) | collective-permute-done | bytes 131104 | tf_op jit(solution)/shard_map/ppermute | solution.py:16
  213.6 11.2 %fusion.141 = f32[16,16,256]{2,1,0:T(8,128)S(1)} fusion(f32[16,16,256]{2,1,0:T(8,128)S(1)} %multiply_subtract_fusion, f32[16,8,256]{2,1,0:T(8,128)S(1)} %collective-permute-done.9, f32[16,8,256]{2,1,0:T(8,128)S(1)} %collective-permute-done.8, f32[]{:T(128)} %bitcast.27, f32[]{:T(128)} %bitcast.26, f32[]{:T(128)} %bitcast.25, f32[]{:T(128)} %bitcast.24, ...), kind=kLoop, calls=%fused_computation.369 | loop fusion | flops 3211264 | bytes 786500 | tf_op jit(solution)/shard_map/add | solution.py:82
  224.9 1.9 collective-permute-start.10
  226.8 6.0 %collective-permute-start.11 = (f32[16,16,8]{2,1,0:T(8,128)S(1)}, f32[16,16,8]{2,1,0:T(8,128)S(1)}, u32[]{:S(2)}, u32[]{:S(2)}) collective-permute-start(f32[16,16,8]{2,1,0:T(8,128)S(1)} %get-tuple-element.35), channel_id=1, source_target_pairs={{16,0},{32,16},{48,32},{64,48},{80,64},{96,80},{112,96},{128,112},... | collective-permute-start | bytes 24584 | tf_op jit(solution)/shard_map/ppermute | solution.py:28
  232.9 0.7 collective-permute-done.10
  233.6 1.8 collective-permute-done.11
  235.4 12.1 %fusion.97 = f32[16,256,16]{1,0,2:T(8,128)S(1)} fusion(f32[16,16,256]{2,1,0:T(8,128)S(1)} %fusion.141, f32[16,16,8]{2,1,0:T(8,128)S(1)} %collective-permute-done.11, f32[16,16,8]{2,1,0:T(8,128)S(1)} %collective-permute-done.10, f32[]{:T(128)} %bitcast.27, f32[]{:T(128)} %bitcast.26, f32[]{:T(128)} %bitcast.25, f32[]{:T(128)} %bitcast.24, f32[]{:T(128)} %bitcast.23, ...), kind=kLoop, calls=%fused_computation.325 | loop fusion | flops 3211264 | bytes 540740
  247.5 0.2 fusion.1
  247.8 12.7 %all_to_all.21 = f32[16,6,1,256]{3,2,1,0:T(1,128)S(1)} all-to-all(f32[16,6,1,256]{3,2,1,0:T(1,128)S(1)} %copy.14), channel_id=1, replica_groups=mesh['tile_0'=16,'tile_1'=2,'tile_2'=2,'mem_0'=2,'mem_1'=8] {'mem_0','me..., dimensions={0} | all-to-all | bytes 196608 | tf_op jit(solution)/shard_map/all_to_all | solution.py:42
  260.6 0.8 reshape_multiply_fusion
  261.5 11.6 %all_to_all.22 = f32[16,6,1,256]{3,2,1,0:T(1,128)S(1)} all-to-all(f32[16,6,1,256]{3,2,1,0:T(1,128)S(1)} %broadcast_in_dim.14), channel_id=1, replica_groups=mesh['tile_0'=16,'tile_1'=2,'tile_2'=2,'mem_0'=2,'mem_1'=8] {'mem_0','me..., dimensions={0} | all-to-all | bytes 196608 | tf_op jit(solution)/shard_map/all_to_all | solution.py:54
  273.3 5.8 %collective-permute-start.12 = (f32[16,8,256]{2,1,0:T(8,128)S(1)}, f32[16,8,256]{2,1,0:T(8,128)S(1)}, u32[]{:S(2)}, u32[]{:S(2)}) collective-permute-start(f32[16,8,256]{2,1,0:T(8,128)S(1)} %get-tuple-element.32), channel_id=1, source_target_pairs={{0,128},{16,144},{32,160},{48,176},{64,192},{80,208},{96,224},{112... | collective-permute-start | bytes 393224 | tf_op jit(solution)/shard_map/ppermute | solution.py:16
  279.1 1.5 collective-permute-start.13
  280.5 1.0 collective-permute-done.12
  281.6 5.3 %collective-permute-done.13 = f32[16,8,256]{2,1,0:T(8,128)S(1)} collective-permute-done((f32[16,8,256]{2,1,0:T(8,128)S(1)}, f32[16,8,256]{2,1,0:T(8,128)S(1)}, u32[]{:S(2)}, u32[]{:S(2)}) %collective-permute-start.13) | collective-permute-done | bytes 131104 | tf_op jit(solution)/shard_map/ppermute | solution.py:16
  286.9 11.2 %fusion.52 = f32[16,16,256]{2,1,0:T(8,128)S(1)} fusion(f32[16,16,256]{2,1,0:T(8,128)S(1)} %bitcast.93, f32[16,8,256]{2,1,0:T(8,128)S(1)} %collective-permute-done.13, f32[16,8,256]{2,1,0:T(8,128)S(1)} %collective-permute-done.12, f32[]{:T(128)} %bitcast.27, f32[]{:T(128)} %bitcast.26, f32[]{:T(128)} %bitcast.25, f32[]{:T(128)} %bitcast.24, f32[]{:T(128)} %bitcast.23, ...), kind=kLoop, calls=%fused_computation.280 | loop fusion | flops 3211264 | bytes 786500 | tf_op jit(solution)/shard_map/add | solution.py:82
  298.2 1.9 collective-permute-start.14
  300.1 6.6 %collective-permute-start.15 = (f32[16,16,8]{2,1,0:T(8,128)S(1)}, f32[16,16,8]{2,1,0:T(8,128)S(1)}, u32[]{:S(2)}, u32[]{:S(2)}) collective-permute-start(f32[16,16,8]{2,1,0:T(8,128)S(1)} %get-tuple-element.31), channel_id=1, source_target_pairs={{16,0},{32,16},{48,32},{64,48},{80,64},{96,80},{112,96},{128,112},... | collective-permute-start | bytes 24584 | tf_op jit(solution)/shard_map/ppermute | solution.py:28
  306.7 0.7 collective-permute-done.14
  307.4 1.8 collective-permute-done.15
  309.2 12.8 %multiply_reduce_fusion = (f32[]{:T(128)}, f32[]{:T(128)}, f32[16,16,256]{2,1,0:T(8,128)S(1)}) fusion(f32[16,16,256]{2,1,0:T(8,128)S(1)} %multiply_subtract_fusion, f32[16,16,8]{2,1,0:T(8,128)S(1)} %collective-permute-done.15, f32[16,16,256]{2,1,0:T(8,128)S(1)} %fusion.52, f32[]{:T(128)} %bitcast.27, f32[]{:T(128)} %bitcast.26, f32[]{:T(128)} %bitcast.25, ...), kind=kLoop, calls=%fused_computation.622 | loop fusion | flops 3538942 | bytes 802892 | tf_op jit(solution)/shard_map/reduce_sum | solution.py:104
  322.0 31.1 %all-reduce = (f32[]{:T(128)}, f32[]{:T(128)}) all-reduce(f32[]{:T(128)} %get-tuple-element.3, f32[]{:T(128)} %get-tuple-element.2), channel_id=1, replica_groups=mesh['tile_0'=16,'tile_1'=2,'tile_2'=2,'mem_0'=2,'mem_1'=8] {'tile_0'}, use_global_device_ids=true, to_apply=%region_15.0 | all-reduce | flops 2 | bytes 16 | tf_op jit(solution)/shard_map/psum | solution.py:63
  353.1 7.1 %all-reduce.8 = (f32[]{:T(128)}, f32[]{:T(128)}) all-reduce(f32[]{:T(128)} %get-tuple-element.6, f32[]{:T(128)} %get-tuple-element.7), channel_id=1, replica_groups=mesh['tile_0'=16,'tile_1'=2,'tile_2'=2,'mem_0'=2,'mem_1'=8] {'tile_1'}, use_global_device_ids=true, to_apply=%region_16.0 | all-reduce | flops 2 | bytes 16 | tf_op jit(solution)/shard_map/psum | solution.py:63
  360.2 3.1 all-reduce.6
  363.2 5.6 %all-reduce.4 = (f32[]{:T(128)}, f32[]{:T(128)}) all-reduce(f32[]{:T(128)} %get-tuple-element.18, f32[]{:T(128)} %get-tuple-element.19), channel_id=1, replica_groups=mesh['tile_0'=16,'tile_1'=2,'tile_2'=2,'mem_0'=2,'mem_1'=8] {'mem_0'}, use_global_device_ids=true, to_apply=%region_18.0 | all-reduce | flops 2 | bytes 16 | tf_op jit(solution)/shard_map/psum | solution.py:63
  368.8 16.1 %all-reduce.2 = (f32[]{:T(128)}, f32[]{:T(128)}) all-reduce(f32[]{:T(128)} %get-tuple-element.14, f32[]{:T(128)} %get-tuple-element.15), channel_id=1, replica_groups=mesh['tile_0'=16,'tile_1'=2,'tile_2'=2,'mem_0'=2,'mem_1'=8] {'mem_1'}, use_global_device_ids=true, to_apply=%region_19.0 | all-reduce | flops 2 | bytes 16 | tf_op jit(solution)/shard_map/psum | solution.py:63
  389.5 0.9 subtract_bitcast_fusion
  (30 shorter events, 1.2 us)
Async XLA Ops:
  0.6 19.6 %copy-start.1 = (f32[1,16,16,256]{3,2,1,0:T(8,128)S(1)}, f32[1,16,16,256]{3,2,1,0:T(8,128)}, u32[]{:S(2)}) copy-start(f32[1,16,16,256]{3,2,1,0:T(8,128)} %param.4) | copy-start | bytes 786436
  1.7 9.4 %collective-permute-start = (f32[16,8,256]{2,1,0:T(8,128)S(1)}, f32[16,8,256]{2,1,0:T(8,128)S(1)}, u32[]{:S(2)}, u32[]{:S(2)}) collective-permute-start(f32[16,8,256]{2,1,0:T(8,128)S(1)} %get-tuple-element.44), channel_id=1, source_target_pairs={{0,128},{16,144},{32,160},{48,176},{64,192},{80,208},{96,224},{112... | collective-permute-start | bytes 393224 | tf_op jit(solution)/shard_map/ppermute | solution.py:16
  7.8 12.4 %collective-permute-start.1 = (f32[16,8,256]{2,1,0:T(8,128)S(1)}, f32[16,8,256]{2,1,0:T(8,128)S(1)}, u32[]{:S(2)}, u32[]{:S(2)}) collective-permute-start(f32[16,8,256]{2,1,0:T(8,128)S(1)} %get-tuple-element.45), channel_id=1, source_target_pairs={{128,0},{144,16},{160,32},{176,48},{192,64},{208,80},{224,96},{240... | collective-permute-start | bytes 393224 | tf_op jit(solution)/shard_map/ppermute | solution.py:16
  31.4 22.9 %copy-start = (bf16[1,16,6,16,256]{4,3,2,1,0:T(8,128)(2,1)S(1)}, bf16[1,16,6,16,256]{4,3,2,1,0:T(8,128)(2,1)}, u32[]{:S(2)}) copy-start(bf16[1,16,6,16,256]{4,3,2,1,0:T(8,128)(2,1)} %param.5) | copy-start | bytes 2359300
  31.5 8.8 %collective-permute-start.2 = (f32[16,16,8]{2,1,0:T(8,128)S(1)}, f32[16,16,8]{2,1,0:T(8,128)S(1)}, u32[]{:S(2)}, u32[]{:S(2)}) collective-permute-start(f32[16,16,8]{2,1,0:T(8,128)S(1)} %get-tuple-element.42), channel_id=1, source_target_pairs={{0,16},{16,32},{32,48},{48,64},{64,80},{80,96},{96,112},{112,128},... | collective-permute-start | bytes 24584 | tf_op jit(solution)/shard_map/ppermute | solution.py:26
  33.6 8.6 %collective-permute-start.3 = (f32[16,16,8]{2,1,0:T(8,128)S(1)}, f32[16,16,8]{2,1,0:T(8,128)S(1)}, u32[]{:S(2)}, u32[]{:S(2)}) collective-permute-start(f32[16,16,8]{2,1,0:T(8,128)S(1)} %get-tuple-element.43), channel_id=1, source_target_pairs={{16,0},{32,16},{48,32},{64,48},{80,64},{96,80},{112,96},{128,112},... | collective-permute-start | bytes 24584 | tf_op jit(solution)/shard_map/ppermute | solution.py:28
  54.3 9.1 %copy-start.2 = (s32[1,2,16]{2,1,0:T(2,128)S(1)}, s32[1,2,16]{2,1,0:T(2,128)}, u32[]{:S(2)}) copy-start(s32[1,2,16]{2,1,0:T(2,128)} %param.7) | copy-start | bytes 388
  55.2 16.7 %all-to-all-start = ((f32[16,6,1,256]{3,2,1,0:T(1,128)}), f32[16,6,1,256]{3,2,1,0:T(1,128)S(1)}, u32[]{:S(2)}, u32[]{:S(2)}) async-start(f32[16,6,1,256]{3,2,1,0:T(1,128)} %copy.12), calls=%async_computation | async-start | bytes 196608 | tf_op jit(solution)/shard_map/all_to_all | solution.py:42
  85.4 9.1 %collective-permute-start.4 = (f32[16,8,256]{2,1,0:T(8,128)S(1)}, f32[16,8,256]{2,1,0:T(8,128)S(1)}, u32[]{:S(2)}, u32[]{:S(2)}) collective-permute-start(f32[16,8,256]{2,1,0:T(8,128)S(1)} %get-tuple-element.40), channel_id=1, source_target_pairs={{0,128},{16,144},{32,160},{48,176},{64,192},{80,208},{96,224},{112... | collective-permute-start | bytes 393224 | tf_op jit(solution)/shard_map/ppermute | solution.py:16
  89.6 12.3 %collective-permute-start.5 = (f32[16,8,256]{2,1,0:T(8,128)S(1)}, f32[16,8,256]{2,1,0:T(8,128)S(1)}, u32[]{:S(2)}, u32[]{:S(2)}) collective-permute-start(f32[16,8,256]{2,1,0:T(8,128)S(1)} %get-tuple-element.41), channel_id=1, source_target_pairs={{128,0},{144,16},{160,32},{176,48},{192,64},{208,80},{224,96},{240... | collective-permute-start | bytes 393224 | tf_op jit(solution)/shard_map/ppermute | solution.py:16
  113.2 8.7 %collective-permute-start.6 = (f32[16,16,8]{2,1,0:T(8,128)S(1)}, f32[16,16,8]{2,1,0:T(8,128)S(1)}, u32[]{:S(2)}, u32[]{:S(2)}) collective-permute-start(f32[16,16,8]{2,1,0:T(8,128)S(1)} %get-tuple-element.38), channel_id=1, source_target_pairs={{0,16},{16,32},{32,48},{48,64},{64,80},{80,96},{96,112},{112,128},... | collective-permute-start | bytes 24584 | tf_op jit(solution)/shard_map/ppermute | solution.py:26
  115.1 8.6 %collective-permute-start.7 = (f32[16,16,8]{2,1,0:T(8,128)S(1)}, f32[16,16,8]{2,1,0:T(8,128)S(1)}, u32[]{:S(2)}, u32[]{:S(2)}) collective-permute-start(f32[16,16,8]{2,1,0:T(8,128)S(1)} %get-tuple-element.39), channel_id=1, source_target_pairs={{16,0},{32,16},{48,32},{64,48},{80,64},{96,80},{112,96},{128,112},... | collective-permute-start | bytes 24584 | tf_op jit(solution)/shard_map/ppermute | solution.py:28
  201.8 7.3 %collective-permute-start.8 = (f32[16,8,256]{2,1,0:T(8,128)S(1)}, f32[16,8,256]{2,1,0:T(8,128)S(1)}, u32[]{:S(2)}, u32[]{:S(2)}) collective-permute-start(f32[16,8,256]{2,1,0:T(8,128)S(1)} %get-tuple-element.36), channel_id=1, source_target_pairs={{0,128},{16,144},{32,160},{48,176},{64,192},{80,208},{96,224},{112... | collective-permute-start | bytes 393224 | tf_op jit(solution)/shard_map/ppermute | solution.py:16
  205.6 8.1 %collective-permute-start.9 = (f32[16,8,256]{2,1,0:T(8,128)S(1)}, f32[16,8,256]{2,1,0:T(8,128)S(1)}, u32[]{:S(2)}, u32[]{:S(2)}) collective-permute-start(f32[16,8,256]{2,1,0:T(8,128)S(1)} %get-tuple-element.37), channel_id=1, source_target_pairs={{128,0},{144,16},{160,32},{176,48},{192,64},{208,80},{224,96},{240... | collective-permute-start | bytes 393224 | tf_op jit(solution)/shard_map/ppermute | solution.py:16
  224.9 8.7 %collective-permute-start.10 = (f32[16,16,8]{2,1,0:T(8,128)S(1)}, f32[16,16,8]{2,1,0:T(8,128)S(1)}, u32[]{:S(2)}, u32[]{:S(2)}) collective-permute-start(f32[16,16,8]{2,1,0:T(8,128)S(1)} %get-tuple-element.34), channel_id=1, source_target_pairs={{0,16},{16,32},{32,48},{48,64},{64,80},{80,96},{96,112},{112,128},... | collective-permute-start | bytes 24584 | tf_op jit(solution)/shard_map/ppermute | solution.py:26
  226.8 8.6 %collective-permute-start.11 = (f32[16,16,8]{2,1,0:T(8,128)S(1)}, f32[16,16,8]{2,1,0:T(8,128)S(1)}, u32[]{:S(2)}, u32[]{:S(2)}) collective-permute-start(f32[16,16,8]{2,1,0:T(8,128)S(1)} %get-tuple-element.35), channel_id=1, source_target_pairs={{16,0},{32,16},{48,32},{64,48},{80,64},{96,80},{112,96},{128,112},... | collective-permute-start | bytes 24584 | tf_op jit(solution)/shard_map/ppermute | solution.py:28
  273.3 8.3 %collective-permute-start.12 = (f32[16,8,256]{2,1,0:T(8,128)S(1)}, f32[16,8,256]{2,1,0:T(8,128)S(1)}, u32[]{:S(2)}, u32[]{:S(2)}) collective-permute-start(f32[16,8,256]{2,1,0:T(8,128)S(1)} %get-tuple-element.32), channel_id=1, source_target_pairs={{0,128},{16,144},{32,160},{48,176},{64,192},{80,208},{96,224},{112... | collective-permute-start | bytes 393224 | tf_op jit(solution)/shard_map/ppermute | solution.py:16
  279.1 7.8 %collective-permute-start.13 = (f32[16,8,256]{2,1,0:T(8,128)S(1)}, f32[16,8,256]{2,1,0:T(8,128)S(1)}, u32[]{:S(2)}, u32[]{:S(2)}) collective-permute-start(f32[16,8,256]{2,1,0:T(8,128)S(1)} %get-tuple-element.33), channel_id=1, source_target_pairs={{128,0},{144,16},{160,32},{176,48},{192,64},{208,80},{224,96},{240... | collective-permute-start | bytes 393224 | tf_op jit(solution)/shard_map/ppermute | solution.py:16
  298.2 9.2 %collective-permute-start.14 = (f32[16,16,8]{2,1,0:T(8,128)S(1)}, f32[16,16,8]{2,1,0:T(8,128)S(1)}, u32[]{:S(2)}, u32[]{:S(2)}) collective-permute-start(f32[16,16,8]{2,1,0:T(8,128)S(1)} %get-tuple-element.30), channel_id=1, source_target_pairs={{0,16},{16,32},{32,48},{48,64},{64,80},{80,96},{96,112},{112,128},... | collective-permute-start | bytes 24584 | tf_op jit(solution)/shard_map/ppermute | solution.py:26
  300.1 9.1 %collective-permute-start.15 = (f32[16,16,8]{2,1,0:T(8,128)S(1)}, f32[16,16,8]{2,1,0:T(8,128)S(1)}, u32[]{:S(2)}, u32[]{:S(2)}) collective-permute-start(f32[16,16,8]{2,1,0:T(8,128)S(1)} %get-tuple-element.31), channel_id=1, source_target_pairs={{16,0},{32,16},{48,32},{64,48},{80,64},{96,80},{112,96},{128,112},... | collective-permute-start | bytes 24584 | tf_op jit(solution)/shard_map/ppermute | solution.py:28
where the time goes:
time: 393 us; the launch traced here: 390 us
  blocking collectives  163 us (41%)
  other arithmetic  98.6 us (25%)
  starting transfers between devices  65.9 us (17%)
  waiting for transfers between devices  51.5 us (13%)
  between operations  7.69 us (2%)
    psum x10, blocking collectives, by_axis(): value = lax.psum(value, axis)  127 us
    add x4, other arithmetic, smooth(): along = along + taps[j] * padded[:, j:j + height, :]  44.8 us
    ppermute x8, waiting for transfers between devices, passed_along(): lax.ppermute(value, axis, [(source, source + steps) for source in range(f...  33.2 us
    reduce_sum x2, other arithmetic, two_products(): jnp.sum(residual * image)  25.5 us
    ppermute x8, starting transfers between devices, passed_along(): lax.ppermute(value, axis, [(source, source + steps) for source in range(f...  25.2 us
    ppermute x4, starting transfers between devices, padded_2(): lax.ppermute(head, axis, [((i + 1) % count, i) for i in range(count)])  24.7 us
    unnamed x2, other arithmetic  24.3 us
    all_to_all x2, blocking collectives, sent_to_all(): return lax.all_to_all(copies, axis, split_axis=0, concat_axis=0, tiled=True)  23.9 us
  transfers between devices with their start and end apart: 17, of which 16 were waited for; matrix products, arithmetic and copies ran while one was open for 0% of the time, Pallas kernels for 0%

commit v1 on v0

v1 whole, which is shorter than its diff:
```python
import functools

import jax
import jax.numpy as jnp
import numpy as np
from jax import lax
from jax.experimental import pallas as pl
from jax.experimental.pallas import tpu as pltpu
from jax.sharding import PartitionSpec as P

TY = 16
TX = 256
VL = 6
KL = 16
HALF = 128
HIGH = lax.Precision.HIGHEST


def filter_constants():
    j = np.arange(-8, 9).astype(np.float64)
    taps = (np.exp(-j * j / 32.0) / np.sqrt(np.sum(np.exp(-j * j / 16.0)))).astype(np.float32)

    def tap(offset):
        return np.where(np.abs(offset) <= 8, taps[np.clip(offset + 8, 0, 16)], np.float32(0))

    y = np.arange(TY)
    own = tap(y[None, :] - y[:, None])
    above = tap(np.arange(-8, 0)[None, :] - y[:, None])
    below = tap(np.arange(16, 24)[None, :] - y[:, None])
    eye = np.eye(8, dtype=np.float32)
    rows = np.concatenate([np.kron(eye, own), np.kron(eye, above), np.kron(eye, below)], axis=1)
    strip = np.concatenate([above, own, below], axis=1)
    x = np.arange(TX)
    columns = tap(x[:, None] - x[None, :])
    c = np.arange(8)
    eye16 = np.eye(16, dtype=np.float32)
    left = np.kron(eye16, tap((c[:, None] - 8) - c[None, :]))
    right = np.kron(eye16, tap((c[:, None] + 8) - c[None, :]))
    spread = (np.arange(16)[:, None] == x[None, :] // 16).astype(np.float32)
    return rows, columns, left, right, strip, spread


def dot(a, b):
    return jnp.dot(a, b, precision=HIGH, preferred_element_type=jnp.float32)


def kernel(
    tiles, tcols, mems,
    src_hbm, pert_hbm, prec_hbm, cov_hbm, rows_hbm, columns_hbm, left_hbm, right_hbm, strip_hbm, spread_hbm,
    w_hbm, res_hbm,
    v0, pert, obsw, cov, rows, columns, left, right, strip, spread, strip_l, strip_r,
    fields, outs, above, below, lhalo, rhalo, packs, inc, rsbuf, agbuf, stat, ar1, ar2, ar3,
    load_sem, store_sem, halo_send, halo_recv, rs_send, rs_recv, ag_send, ag_recv, ar_send, ar_recv,
):
    t = lax.axis_index("tile")
    m = lax.axis_index("mem")
    depth = tiles // 4

    def at_tile(offset):
        return {"tile": lax.rem(t + (offset + tiles), tiles), "mem": m}

    def at_mem(offset):
        return {"tile": t, "mem": lax.rem(m + offset, mems)}

    def at_quad(offset):
        q = lax.rem(t, 4)
        return {"tile": t - q + lax.rem(q + offset, 4), "mem": m}

    def at_depth(offset):
        return {"tile": lax.rem(t + 4 * offset, tiles), "mem": m}

    loads = []
    for i, (source, target) in enumerate(
        (
            (src_hbm.at[0], v0), (pert_hbm.at[0], pert), (prec_hbm.at[0], obsw), (cov_hbm.at[0], cov),
            (rows_hbm, rows), (columns_hbm, columns), (left_hbm, left), (right_hbm, right),
            (strip_hbm, strip), (spread_hbm, spread),
        )
    ):
        copy = pltpu.make_async_copy(source, target, load_sem.at[i])
        copy.start()
        loads.append(copy)

    neighbours = (tcols, -tcols, 1, -1, tcols + 1, -tcols - 1, tcols - 1, 1 - tcols)
    barrier = pltpu.get_barrier_semaphore()
    greeted = (
        [at_tile(d) for d in neighbours]
        + [at_mem(d) for d in range(1, mems)]
        + [at_quad(d) for d in range(1, 4)]
        + [at_depth(d) for d in range(1, depth)]
    )
    for device in greeted:
        pl.semaphore_signal(barrier, inc=1, device_id=device, device_id_type=pl.DeviceIdType.MESH)
    pl.semaphore_wait(barrier, len(greeted))

    sends = []

    def remote(source, target, send, recv, device):
        copy = pltpu.make_async_remote_copy(
            src_ref=source, dst_ref=target, send_sem=send, recv_sem=recv,
            device_id=device, device_id_type=pl.DeviceIdType.MESH,
        )
        copy.start()
        sends.append(copy)
        return copy

    lane = lax.broadcasted_iota(jnp.int32, (TY, HALF), 1)

    def send_rows(n, source):
        return [
            remote(source.at[:, pl.ds(8, 8), :], above.at[n], halo_send.at[n, 0], halo_recv.at[n, 0], at_tile(tcols)),
            remote(source.at[:, pl.ds(0, 8), :], below.at[n], halo_send.at[n, 1], halo_recv.at[n, 1], at_tile(-tcols)),
        ]

    def send_edges(n, field):
        packed_l = jnp.zeros((TY, HALF), jnp.float32)
        packed_r = jnp.zeros((TY, HALF), jnp.float32)
        for k in range(KL):
            here = lane // 8 == k
            value_l = field[k, :, 0:HALF]
            value_r = field[k, :, HALF:TX]
            value_l = pltpu.roll(value_l, 8 * k, 1) if k else value_l
            value_r = pltpu.roll(value_r, 8 * k + 8, 1) if k < KL - 1 else value_r
            packed_l = jnp.where(here, value_l, packed_l)
            packed_r = jnp.where(here, value_r, packed_r)
        packs[n, 0] = packed_l
        packs[n, 1] = packed_r
        pl_ref, pr_ref = packs.at[n, 0], packs.at[n, 1]
        lh, rh = lhalo.at[n], rhalo.at[n]
        s, r = halo_send, halo_recv
        top, bottom = pl.ds(0, 8), pl.ds(8, 8)
        return [
            remote(pr_ref, lh.at[pl.ds(8, 16), :], s.at[n, 2], r.at[n, 2], at_tile(1)),
            remote(pl_ref, rh.at[pl.ds(8, 16), :], s.at[n, 3], r.at[n, 3], at_tile(-1)),
            remote(pr_ref.at[bottom, :], lh.at[pl.ds(0, 8), :], s.at[n, 4], r.at[n, 4], at_tile(tcols + 1)),
            remote(pl_ref.at[top, :], rh.at[pl.ds(24, 8), :], s.at[n, 5], r.at[n, 5], at_tile(-tcols - 1)),
            remote(pl_ref.at[bottom, :], rh.at[pl.ds(0, 8), :], s.at[n, 6], r.at[n, 6], at_tile(tcols - 1)),
            remote(pr_ref.at[top, :], lh.at[pl.ds(24, 8), :], s.at[n, 7], r.at[n, 7], at_tile(1 - tcols)),
        ]

    def smooth(n, field, target, copies):
        for copy in copies:
            copy.wait_recv()
        edge_l = dot(dot(strip_l[...], lhalo[n]), left[...])
        edge_r = dot(dot(strip_r[...], rhalo[n]), right[...])
        for group in range(2):
            ks = pl.ds(8 * group, 8)
            stacked = jnp.concatenate(
                [
                    field[ks].reshape(128, TX),
                    above[n, ks].reshape(64, TX),
                    below[n, ks].reshape(64, TX),
                ],
                axis=0,
            )
            filtered = dot(dot(rows[...], stacked), columns[...])
            for i in range(8):
                k = 8 * group + i
                part = filtered[TY * i : TY * i + TY]
                low, high = part[:, :HALF], part[:, HALF:]
                add_l = pltpu.roll(edge_l, HALF - 8 * k, 1) if k else edge_l
                add_r = pltpu.roll(edge_r, 120 - 8 * k, 1) if k < KL - 1 else edge_r
                target[k, :, 0:HALF] = low + jnp.where(lane < 8, add_l, 0.0)
                target[k, :, HALF:TX] = high + jnp.where(lane >= 120, add_r, 0.0)

    def increment(n, field):
        def body(k, totals):
            value = field[k]
            return tuple(totals[v] + pert[k, v].astype(jnp.float32) * value for v in range(VL))

        zero = jnp.zeros((TY, TX), jnp.float32)
        totals = lax.fori_loop(0, KL, body, (zero,) * VL)
        for v in range(VL):
            for h in range(2):
                inc[n, h, pl.ds(v, TY, stride=8), :] = totals[v][:, HALF * h : HALF * h + HALF]
        rows_of = lambda y: pl.ds(pl.multiple_of(8 * y, 8), 8)
        copies = []
        for d in range(1, mems):
            there = lax.rem(m + d, mems)
            for piece in range(TY // mems):
                copies.append(
                    remote(
                        inc.at[n, :, rows_of(there * (TY // mems) + piece), :], rsbuf.at[n, d - 1, piece],
                        rs_send.at[n, d - 1, piece], rs_recv.at[n, d - 1, piece], at_mem(d),
                    )
                )
        for copy in copies:
            copy.wait_recv()
        copies = []
        for piece in range(TY // mems):
            mine = rows_of(m * (TY // mems) + piece)
            total = inc[n, :, mine, :]
            for d in range(1, mems):
                total = total + rsbuf[n, d - 1, piece]
            agbuf[n, :, mine, :] = total
        for d in range(1, mems):
            for piece in range(TY // mems):
                mine = rows_of(m * (TY // mems) + piece)
                copies.append(
                    remote(
                        agbuf.at[n, :, mine, :], agbuf.at[n, :, mine, :],
                        ag_send.at[n, d - 1, piece], ag_recv.at[n, d - 1, piece], at_mem(d),
                    )
                )
        for copy in copies:
            copy.wait_recv()

    def adjoint(n, target):
        weighted = []
        for v in range(VL):
            halves = [agbuf[n, h, pl.ds(v, TY, stride=8), :] for h in range(2)]
            weighted.append(obsw[v] * jnp.concatenate(halves, axis=1))

        def body(k, carry):
            total = pert[k, 0].astype(jnp.float32) * weighted[0]
            for v in range(1, VL):
                total = total + pert[k, v].astype(jnp.float32) * weighted[v]
            target[k] = total
            return carry

        lax.fori_loop(0, KL, body, 0)

    g0, v1, g1, u = fields.at[0], fields.at[1], fields.at[2], fields.at[3]
    v2 = fields.at[4]

    copies = send_rows(0, src_hbm.at[0])
    loads[0].wait()
    copies += send_edges(0, v0)
    for copy in loads[1:]:
        copy.wait()

    def known(position, least, below_that):
        return jnp.logical_and(position >= least, position < below_that).astype(jnp.float32)

    def flags(offset):
        s = lax.rem(t + (offset + tiles), tiles)
        return known(s, tcols, tiles), known(s, 0, tiles - tcols)

    top, bottom = flags(0)
    rows[:, 128:192] = rows[:, 128:192] * top
    rows[:, 192:256] = rows[:, 192:256] * bottom
    column = lax.broadcasted_iota(jnp.int32, (TY, 32), 1)
    for offset, target in ((-1, strip_l), (1, strip_r)):
        top, bottom = flags(offset)
        scale = jnp.where(column < 8, top, jnp.where(column >= 24, bottom, 1.0))
        target[...] = strip[...] * scale
    mask = dot(cov[...].astype(jnp.float32), spread[...])
    mask = jnp.concatenate([jnp.broadcast_to(mask[i : i + 1], (8, TX)) for i in range(2)], axis=0)
    for v in range(VL):
        obsw[v] = obsw[v] * mask
    inc[...] = jnp.zeros_like(inc)

    smooth(0, v0, u, copies)
    increment(0, u)
    adjoint(0, g0)
    copies = send_rows(1, g0)
    copies += send_edges(1, g0)
    smooth(1, g0, v1, copies)
    copies = send_rows(2, v1)
    copies += send_edges(2, v1)
    smooth(2, v1, u, copies)
    increment(1, u)
    adjoint(1, g1)
    copies = send_rows(3, g1)
    copies += send_edges(3, g1)
    smooth(3, g1, v2, copies)

    def gram(k, totals):
        a, b, c = v0[k], v1[k], v2[k]
        terms = (a * a, a * b, b * b, a * c, b * c)
        return tuple(total + term for total, term in zip(totals, terms))

    totals = lax.fori_loop(0, KL, gram, (jnp.zeros((TY, TX), jnp.float32),) * 5)
    lane1 = lax.broadcasted_iota(jnp.int32, (1, HALF), 1)
    row = jnp.zeros((1, HALF), jnp.float32)
    for i, total in enumerate(totals):
        line = jnp.sum(total, axis=0, keepdims=True)
        row = jnp.where(lane1 == i, jnp.sum(line, axis=1, keepdims=True), row)
    base = 0
    for stage, (buffer, count, place) in enumerate(((ar1, 4, at_quad), (ar2, mems, at_mem), (ar3, depth, at_depth))):
        stat[stage] = row
        copies = [
            remote(stat.at[stage], buffer.at[d - 1], ar_send.at[base + d], ar_recv.at[base + d], place(d))
            for d in range(1, count)
        ]
        base += count
        for copy in copies:
            copy.wait_recv()
        for d in range(1, count):
            row = row + buffer[d - 1]

    aa, ab, bb, ac, bc = (
        jnp.sum(jnp.where(lane1 == i, row, 0.0), axis=1, keepdims=True) for i in range(5)
    )
    first = aa / (aa + ab)
    rest = ab / (aa + ab)
    after = rest * rest * aa - 2.0 * rest * first * ab + first * first * bb
    along = rest + after / aa
    curved = along * along * (aa + ab) - along * first * (2.0 * ab + bb + ac) + first * first * (bb + bc)
    second = after / curved
    w0, w1 = first + second * along, -(second * first)
    q0, q1, q2 = rest - second * along, -first - second * (along - first), second * first
    for k in range(KL):
        a, b, c = v0[k], v1[k], v2[k]
        outs[0, k] = w0 * a + w1 * b
        outs[1, k] = q0 * a + q1 * b + q2 * c
    stores = [
        pltpu.make_async_copy(outs.at[i], target.at[0], store_sem.at[i]) for i, target in enumerate((w_hbm, res_hbm))
    ]
    for copy in stores:
        copy.start()
    for copy in sends:
        copy.wait_send()
    for copy in stores:
        copy.wait()


def local(tiles, tcols, mems, right_side, perturbations, precision, covered):
    constants = [jnp.asarray(array) for array in filter_constants()]
    field = jax.ShapeDtypeStruct((1, KL, TY, TX), jnp.float32)
    f32 = jnp.float32
    pieces = TY // mems
    scratch = [
        pltpu.VMEM((KL, TY, TX), f32),
        pltpu.VMEM((KL, VL, TY, TX), jnp.bfloat16),
        pltpu.VMEM((VL, TY, TX), f32),
        pltpu.VMEM((2, 16), jnp.int32),
        pltpu.VMEM((128, 256), f32),
        pltpu.VMEM((256, 256), f32),
        pltpu.VMEM((128, 128), f32),
        pltpu.VMEM((128, 128), f32),
        pltpu.VMEM((16, 32), f32),
        pltpu.VMEM((16, 256), f32),
        pltpu.VMEM((16, 32), f32),
        pltpu.VMEM((16, 32), f32),
        pltpu.VMEM((5, KL, TY, TX), f32),
        pltpu.VMEM((2, KL, TY, TX), f32),
        pltpu.VMEM((4, KL, 8, TX), f32),
        pltpu.VMEM((4, KL, 8, TX), f32),
        pltpu.VMEM((4, 32, HALF), f32),
        pltpu.VMEM((4, 32, HALF), f32),
        pltpu.VMEM((4, 2, TY, HALF), f32),
        pltpu.VMEM((2, 2, 128, HALF), f32),
        pltpu.VMEM((2, mems - 1, pieces, 2, 8, HALF), f32),
        pltpu.VMEM((2, 2, 128, HALF), f32),
        pltpu.VMEM((3, 1, HALF), f32),
        pltpu.VMEM((3, 1, HALF), f32),
        pltpu.VMEM((mems - 1, 1, HALF), f32),
        pltpu.VMEM((tiles // 4 - 1, 1, HALF), f32),
        pltpu.SemaphoreType.DMA((10,)),
        pltpu.SemaphoreType.DMA((2,)),
        pltpu.SemaphoreType.DMA((4, 8)),
        pltpu.SemaphoreType.DMA((4, 8)),
        pltpu.SemaphoreType.DMA((2, mems - 1, pieces)),
        pltpu.SemaphoreType.DMA((2, mems - 1, pieces)),
        pltpu.SemaphoreType.DMA((2, mems - 1, pieces)),
        pltpu.SemaphoreType.DMA((2, mems - 1, pieces)),
        pltpu.SemaphoreType.DMA((4 + mems + tiles // 4,)),
        pltpu.SemaphoreType.DMA((4 + mems + tiles // 4,)),
    ]
    return pl.pallas_call(
        functools.partial(kernel, tiles, tcols, mems),
        out_shape=(field, field),
        in_specs=[pl.BlockSpec(memory_space=pl.ANY)] * 10,
        out_specs=(pl.BlockSpec(memory_space=pl.ANY),) * 2,
        scratch_shapes=scratch,
        compiler_params=pltpu.CompilerParams(
            collective_id=0, has_side_effects=True, vmem_limit_bytes=40 * 2**20
        ),
        name="conjugate_gradients",
    )(right_side, perturbations, precision, covered, *constants)


def solution(mesh, tcols=8):
    in_specs = (
        P("tile", "mem", None, None),
        P("tile", "mem", None, None, None),
        P("tile", None, None, None),
        P("tile", None, None),
    )
    out_specs = (P("tile", "mem", None, None),) * 2
    body = functools.partial(local, mesh.shape["tile"], tcols, mesh.shape["mem"])
    return jax.shard_map(body, mesh=mesh, in_specs=in_specs, out_specs=out_specs, check_vma=False)
```

time: 393 us -> 120 us (0.31)
  the two profiles are of different devices: /device:TPU:64 before, /device:TPU:8 now
where the time goes in v1:
time: 120 us; the launch traced here: 119 us
  Pallas kernels  109 us (91%)
  local copies, waits for them, and re-layouts  10 us (8%)
    pallas_call x1, Pallas kernels, local(): pl.pallas_call(functools.partial(kernel, tiles, tcols, mems), out_shape=(...  109 us
    unnamed x22, local copies, waits for them, and re-layouts  10 us

profile of v1, /device:TPU:8, one launch (start us, length us, event | category | flops | bytes accessed | tf_op | source)
XLA Modules:
  0.0 119.4 jit_solution(13314063983351159179)
XLA Ops:
  0.6 0.0 copy-start
  0.6 1.1 copy-done
  1.8 0.0 copy-start.1
  1.8 0.9 copy-done.1
  2.7 0.0 copy-start.2
  2.7 0.9 copy-done.2
  3.7 0.0 copy-start.3
  3.7 0.9 copy-done.3
  4.6 0.0 copy-start.4
  4.6 0.9 copy-done.4
  5.5 0.0 copy-start.5
  5.5 0.8 copy-done.5
  6.3 0.0 copy-start.6
  6.3 0.8 copy-done.6
  7.1 0.0 copy-start.7
  7.1 0.7 copy-done.7
  7.9 0.0 copy-start.8
  7.9 0.7 copy-done.8
  8.6 0.0 copy-start.9
  8.6 0.7 copy-done.9
  9.2 108.7 %conjugate_gradients.1 = (f32[1,16,16,256]{3,2,1,0:T(8,128)S(1)}, f32[1,16,16,256]{3,2,1,0:T(8,128)S(1)}) custom-call(f32[1,16,16,256]{3,2,1,0:T(8,128)S(1)} %copy-done.1, bf16[1,16,6,16,256]{4,3,2,1,0:T(8,128)(2,1)S(1)} %copy-done, f32[1,6,16,256]{3,2,1,0:T(8,128)S(1)} %copy-done.4, s32[1,2,16]{2,1,0:T(2,128)S(1)} %copy-done.9, f32[128,256]{1,0:T(8,128)S(1)} %copy-done.3, ...), custom_call_target="tpu_custom_call" | custom-call | tf_op jit(solution)/shard_map/conjugate_gradients/pallas_call | solution.py:361
  118.0 0.7 copy.14
  118.7 0.7 copy.15
Async XLA Ops:
  0.6 1.1 copy-start
  1.8 0.9 copy-start.1
  2.7 0.9 copy-start.2
  3.7 0.9 copy-start.3
  4.6 0.9 copy-start.4
  5.5 0.8 copy-start.5
  6.3 0.8 copy-start.6
  7.1 0.7 copy-start.7
  7.9 0.7 copy-start.8
  8.6 0.7 copy-start.9

commit v2 on v1

v2 whole, which is shorter than its diff:
```python
import functools

import jax
import jax.numpy as jnp
import numpy as np
from jax import lax
from jax.experimental import pallas as pl
from jax.experimental.pallas import tpu as pltpu
from jax.sharding import PartitionSpec as P

TY = 16
TX = 256
VL = 6
KL = 16
HALF = 128
GROUPS = 2
KG = KL // GROUPS
F32 = jnp.float32
BF16 = jnp.bfloat16


def three(matrix, dim):
    high = matrix.astype(BF16)
    low = (matrix - high.astype(np.float32)).astype(BF16)
    return np.concatenate([high, low, high] if dim else [high, high, low], axis=dim)


def filter_constants():
    j = np.arange(-8, 9).astype(np.float64)
    taps = (np.exp(-j * j / 32.0) / np.sqrt(np.sum(np.exp(-j * j / 16.0)))).astype(np.float32)

    def tap(offset):
        return np.where(np.abs(offset) <= 8, taps[np.clip(offset + 8, 0, 16)], np.float32(0))

    y = np.arange(TY)
    own = tap(y[None, :] - y[:, None])
    above = tap(np.arange(-8, 0)[None, :] - y[:, None])
    below = tap(np.arange(16, 24)[None, :] - y[:, None])
    eye = np.eye(KG, dtype=np.float32)
    rows = np.concatenate(
        [three(np.kron(eye, own), 1), three(np.concatenate([np.kron(eye, above), np.kron(eye, below)], axis=1), 1)], axis=1
    )
    strip = three(np.concatenate([above, own, below], axis=1), 1)
    x = np.arange(TX)
    columns = three(tap(x[:, None] - x[None, :]), 0)
    c = np.arange(8)
    eye16 = np.eye(16, dtype=np.float32)
    none = np.zeros((HALF, HALF), np.float32)
    left = np.kron(eye16, tap((c[:, None] - 8) - c[None, :]))
    right = np.kron(eye16, tap((c[:, None] + 8) - c[None, :]))
    edges = three(np.block([[left, none], [none, right]]), 0)
    spread = (np.arange(16)[:, None] == x[None, :] // 16).astype(np.float32)
    return rows, columns, edges, strip, spread


def split(value):
    high = value.astype(BF16)
    return high, (value - high.astype(F32)).astype(BF16)


def left_product(constant, value):
    high, low = split(value)
    return jnp.dot(constant, jnp.concatenate([high, high, low], axis=0), preferred_element_type=F32)


def right_product(value, constant):
    high, low = split(value)
    return jnp.dot(jnp.concatenate([high, low, high], axis=1), constant, preferred_element_type=F32)


def kernel(
    tiles, tcols, mems,
    src_hbm, pert_hbm, prec_hbm, cov_hbm, rows_hbm, columns_hbm, edges_hbm, strip_hbm, spread_hbm,
    w_out, r_out,
    v0, pert, obsw, cov, rows, columns, edges, strip, spread, fmask, tmask,
    fields, above, below, ehalo, packs, inc, rsbuf, agbuf, stat, ar1, ar2,
    load_sem, halo_send, halo_recv, rs_send, rs_recv, ag_send, ag_recv, ar_send, ar_recv,
):
    t = lax.axis_index("tile")
    m = lax.axis_index("mem")
    depth = tiles // 4

    def at_tile(offset):
        return {"tile": lax.rem(t + (offset + tiles), tiles), "mem": m}

    def at_mem(offset):
        return {"tile": t, "mem": lax.rem(m + offset, mems)}

    def at_plane(offset):
        q = lax.rem(t, 4)
        return {"tile": t - q + lax.rem(q + offset // mems, 4), "mem": lax.rem(m + offset % mems, mems)}

    def at_depth(offset):
        return {"tile": lax.rem(t + 4 * offset, tiles), "mem": m}

    neighbours = (tcols, -tcols, 1, -1, tcols + 1, -tcols - 1, tcols - 1, 1 - tcols)
    barrier = pltpu.get_barrier_semaphore()
    greeted = [at_tile(d) for d in neighbours] + [at_mem(d) for d in range(1, mems)]
    for device in greeted:
        pl.semaphore_signal(barrier, inc=1, device_id=device, device_id_type=pl.DeviceIdType.MESH)

    loads = []
    for i, (source, target) in enumerate(
        (
            (src_hbm.at[0], v0), (pert_hbm.at[0], pert), (prec_hbm.at[0], obsw), (cov_hbm.at[0], cov),
            (rows_hbm, rows), (columns_hbm, columns), (edges_hbm, edges), (strip_hbm, strip), (spread_hbm, spread),
        )
    ):
        copy = pltpu.make_async_copy(source, target, load_sem.at[i])
        copy.start()
        loads.append(copy)
    pl.semaphore_wait(barrier, len(greeted))

    sends = []

    def remote(source, target, send, recv, device):
        copy = pltpu.make_async_remote_copy(
            src_ref=source, dst_ref=target, send_sem=send, recv_sem=recv,
            device_id=device, device_id_type=pl.DeviceIdType.MESH,
        )
        copy.start()
        sends.append(copy)
        return copy

    lane = lax.broadcasted_iota(jnp.int32, (TY, HALF), 1)
    arrivals = [[[] for g in range(GROUPS)] for n in range(4)]

    def members(g):
        return pl.ds(KG * g, KG)

    def send_rows(n, g, source):
        s, r = halo_send.at[n, g], halo_recv.at[n, g]
        arrivals[n][g] += [
            remote(source.at[members(g), pl.ds(8, 8), :], above.at[n, g], s.at[0], r.at[0], at_tile(tcols)),
            remote(source.at[members(g), pl.ds(0, 8), :], below.at[n, g], s.at[1], r.at[1], at_tile(-tcols)),
        ]

    def send_edges(n, g, field):
        packed_l = jnp.zeros((TY, HALF), F32)
        packed_r = jnp.zeros((TY, HALF), F32)
        for i in range(KG):
            here = lane // 8 == i
            value_l = field[KG * g + i, :, 0:HALF]
            value_l = pltpu.roll(value_l, 8 * i, 1) if i else value_l
            value_r = pltpu.roll(field[KG * g + i, :, HALF:TX], 8 * i + 8, 1)
            packed_l = jnp.where(here, value_l, packed_l)
            packed_r = jnp.where(here, value_r, packed_r)
        packs[n, g, :, 0:HALF] = packed_l
        packs[n, g, :, HALF:TX] = packed_r
        left, right = pl.ds(0, HALF), pl.ds(HALF, HALF)
        top, bottom, whole = pl.ds(0, 8), pl.ds(8, 8), pl.ds(0, TY)
        for i, (rows_sent, side, place, half, offset) in enumerate(
            (
                (bottom, right, 0, left, tcols + 1), (top, left, 24, right, -tcols - 1),
                (bottom, left, 0, right, tcols - 1), (top, right, 24, left, 1 - tcols),
                (whole, right, 8, left, 1), (whole, left, 8, right, -1),
            )
        ):
            height = TY if place == 8 else 8
            arrivals[n][g].append(
                remote(
                    packs.at[n, g, rows_sent, side], ehalo.at[n, g, pl.ds(place, height), half],
                    halo_send.at[n, g, 2 + i], halo_recv.at[n, g, 2 + i], at_tile(offset),
                )
            )

    def flags(offset):
        s = lax.rem(t + (offset + tiles), tiles)
        return (s >= tcols).astype(F32), (s < tiles - tcols).astype(F32)

    here_top, here_bottom = flags(0)

    def smooth(n, g, field, target):
        partial = left_product(rows[:, : 3 * HALF], field[members(g)].reshape(KG * TY, TX))
        for copy in arrivals[n][g]:
            copy.wait_recv()
        edge = right_product(left_product(strip[...], ehalo[n, g] * fmask[...]), edges[...])
        halo = jnp.concatenate(
            [above[n, g].reshape(KG * 8, TX) * here_top, below[n, g].reshape(KG * 8, TX) * here_bottom], axis=0
        )
        filtered = right_product(partial + left_product(rows[:, 3 * HALF :], halo), columns[...])
        edge_l, edge_r = edge[:, :HALF], edge[:, HALF:]
        for i in range(KG):
            k = KG * g + i
            part = filtered[TY * i : TY * i + TY]
            add_l = pltpu.roll(edge_l, HALF - 8 * i, 1) if i else edge_l
            add_r = pltpu.roll(edge_r, 120 - 8 * i, 1)
            target[k, :, 0:HALF] = part[:, :HALF] + jnp.where(lane < 8, add_l, 0.0)
            target[k, :, HALF:TX] = part[:, HALF:] + jnp.where(lane >= 120, add_r, 0.0)

    def corners(n, g):
        return right_product(left_product(strip[...], ehalo[n, g] * tmask[...]), edges[...])

    def gathered(field, g, totals):
        def body(k, totals):
            value = field[k]
            return tuple(totals[v] + pert[k, v].astype(F32) * value for v in range(VL))

        return lax.fori_loop(KG * g, KG * g + KG, body, totals)

    pieces = TY // mems

    def rows_of(y):
        return pl.ds(pl.multiple_of(8 * y, 8), 8)

    def exchange(n, totals, meanwhile):
        for v in range(VL):
            for h in range(2):
                inc[n, h, pl.ds(v, TY, stride=8), :] = totals[v][:, HALF * h : HALF * h + HALF]
        copies = []
        for d in range(1, mems):
            there = lax.rem(m + d, mems)
            for piece in range(pieces):
                copies.append(
                    remote(
                        inc.at[n, :, rows_of(there * pieces + piece), :], rsbuf.at[n, d - 1, piece],
                        rs_send.at[n, d - 1, piece], rs_recv.at[n, d - 1, piece], at_mem(d),
                    )
                )
        result = meanwhile()
        for copy in copies:
            copy.wait_recv()
        copies = []
        for piece in range(pieces):
            mine = rows_of(m * pieces + piece)
            total = inc[n, :, mine, :]
            for d in range(1, mems):
                total = total + rsbuf[n, d - 1, piece]
            agbuf[n, :, mine, :] = total
        for d in range(1, mems):
            for piece in range(pieces):
                mine = rows_of(m * pieces + piece)
                copies.append(
                    remote(
                        agbuf.at[n, :, mine, :], agbuf.at[n, :, mine, :],
                        ag_send.at[n, d - 1, piece], ag_recv.at[n, d - 1, piece], at_mem(d),
                    )
                )
        for copy in copies:
            copy.wait_recv()
        return result

    def weighted(n):
        values = []
        for v in range(VL):
            halves = [agbuf[n, h, pl.ds(v, TY, stride=8), :] for h in range(2)]
            values.append(obsw[v] * jnp.concatenate(halves, axis=1))
        return values

    def adjoint(g, values, target):
        def body(k, carry):
            total = pert[k, 0].astype(F32) * values[0]
            for v in range(1, VL):
                total = total + pert[k, v].astype(F32) * values[v]
            target[k] = total
            return carry

        lax.fori_loop(KG * g, KG * g + KG, body, 0)

    g0, g1, u0, u1, v1, v2 = (fields.at[i] for i in range(6))
    zeros = (jnp.zeros((TY, TX), F32),) * VL

    send_rows(0, 0, src_hbm.at[0])
    loads[0].wait()
    for g in range(GROUPS):
        send_edges(0, g, v0)
    for g in range(1, GROUPS):
        send_rows(0, g, src_hbm.at[0])
    for copy in loads[1:]:
        copy.wait()
    row8 = lax.broadcasted_iota(jnp.int32, (32, TX), 0)
    is_left = lax.broadcasted_iota(jnp.int32, (32, TX), 1) < HALF

    def masked(top, bottom):
        return jnp.where(row8 < 8, top, jnp.where(row8 >= 24, bottom, 1.0))

    mask = jnp.where(is_left, masked(*flags(-1)), masked(*flags(1)))
    fmask[...] = mask
    tmask[...] = masked(here_top, here_bottom) - mask
    mask = jnp.dot(cov[...].astype(F32), spread[...], preferred_element_type=F32)
    mask = jnp.concatenate([jnp.broadcast_to(mask[i : i + 1], (8, TX)) for i in range(2)], axis=0)
    for v in range(VL):
        obsw[v] = obsw[v] * mask
    inc[...] = jnp.zeros_like(inc)

    totals = zeros
    for g in range(GROUPS):
        smooth(0, g, v0, u0)
        totals = gathered(u0, g, totals)
    twist_0 = exchange(0, totals, lambda: [corners(0, g) for g in range(GROUPS)])
    values = weighted(0)
    for g in range(GROUPS):
        adjoint(g, values, g0)
        send_edges(1, g, g0)
        send_rows(1, g, g0)
    for g in range(GROUPS):
        smooth(1, g, g0, v1)
        send_edges(2, g, v1)
        send_rows(2, g, v1)
    totals = zeros
    for g in range(GROUPS):
        smooth(2, g, v1, u1)
        totals = gathered(u1, g, totals)

    def lines(totals):
        return [jnp.sum(total[:, :HALF] + total[:, HALF:], axis=0, keepdims=True) for total in totals]

    def known_products():
        def body(k, totals):
            a, b = v0[k], v1[k]
            return totals[0] + a * a, totals[1] + a * b, totals[2] + b * b

        return [corners(2, g) for g in range(GROUPS)], lines(lax.fori_loop(0, KL, body, zeros[:3]))

    twist_1, sums = exchange(1, totals, known_products)
    values = weighted(1)
    for g in range(GROUPS):
        adjoint(g, values, g1)
        send_edges(3, g, g1)
        send_rows(3, g, g1)

    def new_products(k, totals):
        return totals[0] + u0[k] * g1[k], totals[1] + u1[k] * g1[k]

    totals = lax.fori_loop(0, KL, new_products, zeros[:2])
    totals = [
        total + sum(twist[g] * packs[3, g] for g in range(GROUPS)) for total, twist in zip(totals, (twist_0, twist_1))
    ]
    sums = sums + lines(totals)
    lane1 = lax.broadcasted_iota(jnp.int32, (1, HALF), 1)
    row = jnp.zeros((1, HALF), F32)
    for i, line in enumerate(sums):
        row = jnp.where(lane1 == i, jnp.sum(line, axis=1, keepdims=True), row)

    def share(stage, buffer, count, place, base):
        stat[stage] = row
        return [
            remote(stat.at[stage], buffer.at[d - 1], ar_send.at[base + d], ar_recv.at[base + d], place(d))
            for d in range(1, count)
        ]

    def collect(buffer, waited):
        for copy in waited:
            copy.wait_recv()
        return row + jnp.sum(buffer[...], axis=0)

    shared = share(0, ar1, 4 * mems, at_plane, 0)
    for g in range(GROUPS - 1):
        smooth(3, g, g1, v2)
    row = collect(ar1, shared)
    shared = share(1, ar2, depth, at_depth, 4 * mems)
    smooth(3, GROUPS - 1, g1, v2)
    row = collect(ar2, shared)

    aa, ab, bb, ac, bc = (
        jnp.sum(jnp.where(lane1 == i, row, 0.0), axis=1, keepdims=True) for i in range(5)
    )
    first = aa / (aa + ab)
    rest = ab / (aa + ab)
    after = rest * rest * aa - 2.0 * rest * first * ab + first * first * bb
    along = rest + after / aa
    curved = along * along * (aa + ab) - along * first * (2.0 * ab + bb + ac) + first * first * (bb + bc)
    second = after / curved
    w0, w1 = first + second * along, -(second * first)
    q0, q1, q2 = rest - second * along, -first - second * (along - first), second * first
    for k in range(KL):
        a, b, c = v0[k], v1[k], v2[k]
        w_out[0, k] = w0 * a + w1 * b
        r_out[0, k] = q0 * a + q1 * b + q2 * c
    for copy in sends:
        copy.wait_send()


def local(tiles, tcols, mems, right_side, perturbations, precision, covered):
    constants = [jnp.asarray(array) for array in filter_constants()]
    field = jax.ShapeDtypeStruct((1, KL, TY, TX), jnp.float32)
    f32 = jnp.float32
    pieces = TY // mems
    scratch = [
        pltpu.VMEM((KL, TY, TX), f32),
        pltpu.VMEM((KL, VL, TY, TX), BF16),
        pltpu.VMEM((VL, TY, TX), f32),
        pltpu.VMEM((2, 16), jnp.int32),
        *[pltpu.VMEM(array.shape, array.dtype) for array in constants],
        pltpu.VMEM((32, TX), f32),
        pltpu.VMEM((32, TX), f32),
        pltpu.VMEM((6, KL, TY, TX), f32),
        pltpu.VMEM((4, GROUPS, KG, 8, TX), f32),
        pltpu.VMEM((4, GROUPS, KG, 8, TX), f32),
        pltpu.VMEM((4, GROUPS, 32, TX), f32),
        pltpu.VMEM((4, GROUPS, TY, TX), f32),
        pltpu.VMEM((2, 2, 128, HALF), f32),
        pltpu.VMEM((2, mems - 1, pieces, 2, 8, HALF), f32),
        pltpu.VMEM((2, 2, 128, HALF), f32),
        pltpu.VMEM((2, 1, HALF), f32),
        pltpu.VMEM((4 * mems - 1, 1, HALF), f32),
        pltpu.VMEM((tiles // 4 - 1, 1, HALF), f32),
        pltpu.SemaphoreType.DMA((9,)),
        pltpu.SemaphoreType.DMA((4, GROUPS, 8)),
        pltpu.SemaphoreType.DMA((4, GROUPS, 8)),
        pltpu.SemaphoreType.DMA((2, mems - 1, pieces)),
        pltpu.SemaphoreType.DMA((2, mems - 1, pieces)),
        pltpu.SemaphoreType.DMA((2, mems - 1, pieces)),
        pltpu.SemaphoreType.DMA((2, mems - 1, pieces)),
        pltpu.SemaphoreType.DMA((4 * mems + tiles // 4,)),
        pltpu.SemaphoreType.DMA((4 * mems + tiles // 4,)),
    ]
    return pl.pallas_call(
        functools.partial(kernel, tiles, tcols, mems),
        out_shape=(field, field),
        in_specs=[pl.BlockSpec(memory_space=pltpu.MemorySpace.HBM)] * 9,
        out_specs=(pl.BlockSpec(memory_space=pltpu.MemorySpace.VMEM),) * 2,
        scratch_shapes=scratch,
        compiler_params=pltpu.CompilerParams(
            collective_id=0, has_side_effects=True, vmem_limit_bytes=40 * 2**20
        ),
        name="conjugate_gradients",
    )(*[pltpu.with_memory_space_constraint(x, pltpu.MemorySpace.HBM) for x in (right_side, perturbations, precision, covered, *constants)])


def solution(mesh, tcols=8):
    in_specs = (
        P("tile", "mem", None, None),
        P("tile", "mem", None, None, None),
        P("tile", None, None, None),
        P("tile", None, None),
    )
    out_specs = (P("tile", "mem", None, None),) * 2
    body = functools.partial(local, mesh.shape["tile"], tcols, mesh.shape["mem"])
    return jax.shard_map(body, mesh=mesh, in_specs=in_specs, out_specs=out_specs, check_vma=False)
```

time: 120 us -> 93.4 us (0.78)
  the two profiles are of different devices: /device:TPU:8 before, /device:TPU:2 now
where the time goes in v2:
time: 93.4 us; the launch traced here: 93.3 us
  Pallas kernels  91.2 us (98%)
  local copies, waits for them, and re-layouts  1.41 us (2%)
    pallas_call x1, Pallas kernels, local(): pl.pallas_call(functools.partial(kernel, tiles, tcols, mems), out_shape=(...  91.2 us

profile of v2, /device:TPU:2, one launch (start us, length us, event | category | flops | bytes accessed | tf_op | source)
XLA Modules:
  0.0 93.3 jit_solution(6328782798520042285)
XLA Ops:
  0.6 91.2 %conjugate_gradients.1 = (f32[1,16,16,256]{3,2,1,0:T(8,128)S(1)}, f32[1,16,16,256]{3,2,1,0:T(8,128)S(1)}) custom-call(f32[1,16,16,256]{3,2,1,0:T(8,128)} %src_hbm.1, bf16[1,16,6,16,256]{4,3,2,1,0:T(8,128)(2,1)} %pert_hbm.1, f32[1,6,16,256]{3,2,1,0:T(8,128)} %prec_hbm.1, s32[1,2,16]{2,1,0:T(2,128)} %cov_hbm.1, bf16[128,768]{1,0:T(8,128)(2,1)} %constant.10.clone.rows_hbm, ...), custom_call_target="tpu_custom_call" | custom-call | tf_op jit(solution)/shard_map/conjugate_gradients/pallas_call | solution.py:408
  91.9 0.7 copy.13
  92.6 0.7 copy.14

commit v3 on v2

--- a/solution.py
+++ b/solution.py
@@ -73,8 +73,8 @@
     src_hbm, pert_hbm, prec_hbm, cov_hbm, rows_hbm, columns_hbm, edges_hbm, strip_hbm, spread_hbm,
     w_out, r_out,
     v0, pert, obsw, cov, rows, columns, edges, strip, spread, fmask, tmask,
-    fields, above, below, ehalo, packs, inc, rsbuf, agbuf, stat, ar1, ar2,
-    load_sem, halo_send, halo_recv, rs_send, rs_recv, ag_send, ag_recv, ar_send, ar_recv,
+    fields, rhalo, ehalo, packs, inc, rsbuf, agbuf, wrows, dinc, dbuf, stat, ar1, ar2,
+    load_sem, send_sem, rows_recv, edges_recv, rs_recv, ag_recv, d_recv, ar_recv,
 ):
     t = lax.axis_index("tile")
     m = lax.axis_index("mem")
@@ -109,33 +109,26 @@
         copy = pltpu.make_async_copy(source, target, load_sem.at[i])
         copy.start()
         loads.append(copy)
-    pl.semaphore_wait(barrier, len(greeted))
-
-    sends = []
-
-    def remote(source, target, send, recv, device):
-        copy = pltpu.make_async_remote_copy(
-            src_ref=source, dst_ref=target, send_sem=send, recv_sem=recv,
+
+    def remote(source, target, kind, recv, device):
+        pltpu.make_async_remote_copy(
+            src_ref=source, dst_ref=target, send_sem=send_sem.at[kind], recv_sem=recv,
             device_id=device, device_id_type=pl.DeviceIdType.MESH,
-        )
-        copy.start()
-        sends.append(copy)
-        return copy
+        ).start()
+
+    def wait_for(buffer, semaphore):
+        pltpu.make_async_copy(buffer, buffer, semaphore).wait()
 
     lane = lax.broadcasted_iota(jnp.int32, (TY, HALF), 1)
-    arrivals = [[[] for g in range(GROUPS)] for n in range(4)]
 
     def members(g):
         return pl.ds(KG * g, KG)
 
     def send_rows(n, g, source):
-        s, r = halo_send.at[n, g], halo_recv.at[n, g]
-        arrivals[n][g] += [
-            remote(source.at[members(g), pl.ds(8, 8), :], above.at[n, g], s.at[0], r.at[0], at_tile(tcols)),
-            remote(source.at[members(g), pl.ds(0, 8), :], below.at[n, g], s.at[1], r.at[1], at_tile(-tcols)),
-        ]
-
-    def send_edges(n, g, field):
+        remote(source.at[members(g), pl.ds(8, 8), :], rhalo.at[n, g, 0], 0, rows_recv.at[n, g], at_tile(tcols))
+        remote(source.at[members(g), pl.ds(0, 8), :], rhalo.at[n, g, 1], 0, rows_recv.at[n, g], at_tile(-tcols))
+
+    def pack_edges(n, g, field):
         packed_l = jnp.zeros((TY, HALF), F32)
         packed_r = jnp.zeros((TY, HALF), F32)
         for i in range(KG):
@@ -147,21 +140,19 @@
             packed_r = jnp.where(here, value_r, packed_r)
         packs[n, g, :, 0:HALF] = packed_l
         packs[n, g, :, HALF:TX] = packed_r
+
+    def send_edges(n, g):
         left, right = pl.ds(0, HALF), pl.ds(HALF, HALF)
         top, bottom, whole = pl.ds(0, 8), pl.ds(8, 8), pl.ds(0, TY)
-        for i, (rows_sent, side, place, half, offset) in enumerate(
-            (
-                (bottom, right, 0, left, tcols + 1), (top, left, 24, right, -tcols - 1),
-                (bottom, left, 0, right, tcols - 1), (top, right, 24, left, 1 - tcols),
-                (whole, right, 8, left, 1), (whole, left, 8, right, -1),
-            )
+        for rows_sent, side, place, half, offset in (
+            (bottom, right, 0, left, tcols + 1), (top, left, 24, right, -tcols - 1),
+            (bottom, left, 0, right, tcols - 1), (top, right, 24, left, 1 - tcols),
+            (whole, right, 8, left, 1), (whole, left, 8, right, -1),
         ):
             height = TY if place == 8 else 8
-            arrivals[n][g].append(
-                remote(
-                    packs.at[n, g, rows_sent, side], ehalo.at[n, g, pl.ds(place, height), half],
-                    halo_send.at[n, g, 2 + i], halo_recv.at[n, g, 2 + i], at_tile(offset),
-                )
+            remote(
+                packs.at[n, g, rows_sent, side], ehalo.at[n, g, pl.ds(place, height), half],
+                1, edges_recv.at[n, g], at_tile(offset),
             )
 
     def flags(offset):
@@ -172,11 +163,11 @@
 
     def smooth(n, g, field, target):
         partial = left_product(rows[:, : 3 * HALF], field[members(g)].reshape(KG * TY, TX))
-        for copy in arrivals[n][g]:
-            copy.wait_recv()
+        wait_for(ehalo.at[n, g], edges_recv.at[n, g])
         edge = right_product(left_product(strip[...], ehalo[n, g] * fmask[...]), edges[...])
+        wait_for(rhalo.at[n, g], rows_recv.at[n, g])
         halo = jnp.concatenate(
-            [above[n, g].reshape(KG * 8, TX) * here_top, below[n, g].reshape(KG * 8, TX) * here_bottom], axis=0
+            [rhalo[n, g, 0].reshape(KG * 8, TX) * here_top, rhalo[n, g, 1].reshape(KG * 8, TX) * here_bottom], axis=0
         )
         filtered = right_product(partial + left_product(rows[:, 3 * HALF :], halo), columns[...])
         edge_l, edge_r = edge[:, :HALF], edge[:, HALF:]
@@ -203,24 +194,44 @@
     def rows_of(y):
         return pl.ds(pl.multiple_of(8 * y, 8), 8)
 
-    def exchange(n, totals, meanwhile):
+    def send_corners(n, twist):
+        def body(i, totals):
+            for g in range(GROUPS):
+                k = KG * g + i
+                turn = lax.rem(HALF - 8 * i, HALF)
+                add_l = jnp.where(lane < 8, pltpu.roll(twist[g][:, :HALF], turn, 1), 0.0)
+                add_r = jnp.where(lane >= 120, pltpu.roll(twist[g][:, HALF:], 120 - 8 * i, 1), 0.0)
+                totals = tuple(
+                    totals[v]
+                    + pert[k, v, :, 0:HALF].astype(F32) * add_l
+                    + pert[k, v, :, HALF:TX].astype(F32) * add_r
+                    for v in range(VL)
+                )
+            return totals
+
+        totals = lax.fori_loop(0, KG, body, (jnp.zeros((TY, HALF), F32),) * VL)
+        for v in range(VL):
+            dinc[n, pl.ds(v, TY, stride=8), :] = totals[v]
+        for d in range(1, mems):
+            for piece in range(pieces):
+                remote(
+                    dinc.at[n, rows_of(lax.rem(m + d, mems) * pieces + piece), :], dbuf.at[n, d - 1, piece],
+                    4, d_recv.at[n], at_mem(d),
+                )
+
+    def exchange(n, totals, meanwhile, ready):
         for v in range(VL):
             for h in range(2):
                 inc[n, h, pl.ds(v, TY, stride=8), :] = totals[v][:, HALF * h : HALF * h + HALF]
-        copies = []
         for d in range(1, mems):
             there = lax.rem(m + d, mems)
             for piece in range(pieces):
-                copies.append(
-                    remote(
-                        inc.at[n, :, rows_of(there * pieces + piece), :], rsbuf.at[n, d - 1, piece],
-                        rs_send.at[n, d - 1, piece], rs_recv.at[n, d - 1, piece], at_mem(d),
-                    )
+                remote(
+                    inc.at[n, :, rows_of(there * pieces + piece), :], rsbuf.at[n, d - 1, piece],
+                    2, rs_recv.at[n], at_mem(d),
                 )
         result = meanwhile()
-        for copy in copies:
-            copy.wait_recv()
-        copies = []
+        wait_for(rsbuf.at[n], rs_recv.at[n])
         for piece in range(pieces):
             mine = rows_of(m * pieces + piece)
             total = inc[n, :, mine, :]
@@ -230,14 +241,9 @@
         for d in range(1, mems):
             for piece in range(pieces):
                 mine = rows_of(m * pieces + piece)
-                copies.append(
-                    remote(
-                        agbuf.at[n, :, mine, :], agbuf.at[n, :, mine, :],
-                        ag_send.at[n, d - 1, piece], ag_recv.at[n, d - 1, piece], at_mem(d),
-                    )
-                )
-        for copy in copies:
-            copy.wait_recv()
+                remote(agbuf.at[n, :, mine, :], agbuf.at[n, :, mine, :], 3, ag_recv.at[n], at_mem(d))
+        result = ready(result)
+        wait_for(rsbuf.at[n], ag_recv.at[n])
         return result
 
     def weighted(n):
@@ -260,12 +266,9 @@
     g0, g1, u0, u1, v1, v2 = (fields.at[i] for i in range(6))
     zeros = (jnp.zeros((TY, TX), F32),) * VL
 
-    send_rows(0, 0, src_hbm.at[0])
     loads[0].wait()
     for g in range(GROUPS):
-        send_edges(0, g, v0)
-    for g in range(1, GROUPS):
-        send_rows(0, g, src_hbm.at[0])
+        pack_edges(0, g, v0)
     for copy in loads[1:]:
         copy.wait()
     row8 = lax.broadcasted_iota(jnp.int32, (32, TX), 0)
@@ -277,25 +280,38 @@
     mask = jnp.where(is_left, masked(*flags(-1)), masked(*flags(1)))
     fmask[...] = mask
     tmask[...] = masked(here_top, here_bottom) - mask
+    for buffer in (inc, wrows, dinc):
+        buffer[...] = jnp.zeros_like(buffer)
     mask = jnp.dot(cov[...].astype(F32), spread[...], preferred_element_type=F32)
     mask = jnp.concatenate([jnp.broadcast_to(mask[i : i + 1], (8, TX)) for i in range(2)], axis=0)
     for v in range(VL):
         obsw[v] = obsw[v] * mask
-    inc[...] = jnp.zeros_like(inc)
-
+        for h in range(2):
+            wrows[h, pl.ds(v, TY, stride=8), :] = obsw[v, :, HALF * h : HALF * h + HALF]
+
+    pl.semaphore_wait(barrier, len(greeted))
+    for g in range(GROUPS):
+        send_edges(0, g)
+    for g in range(GROUPS):
+        send_rows(0, g, src_hbm.at[0])
     totals = zeros
     for g in range(GROUPS):
         smooth(0, g, v0, u0)
         totals = gathered(u0, g, totals)
-    twist_0 = exchange(0, totals, lambda: [corners(0, g) for g in range(GROUPS)])
+    def corner_sums(n):
+        send_corners(n, [corners(2 * n, g) for g in range(GROUPS)])
+
+    exchange(0, totals, lambda: corner_sums(0), lambda result: None)
     values = weighted(0)
     for g in range(GROUPS):
         adjoint(g, values, g0)
-        send_edges(1, g, g0)
+        pack_edges(1, g, g0)
+        send_edges(1, g)
         send_rows(1, g, g0)
     for g in range(GROUPS):
         smooth(1, g, g0, v1)
-        send_edges(2, g, v1)
+        pack_edges(2, g, v1)
+        send_edges(2, g)
         send_rows(2, g, v1)
     totals = zeros
     for g in range(GROUPS):
@@ -310,47 +326,53 @@
             a, b = v0[k], v1[k]
             return totals[0] + a * a, totals[1] + a * b, totals[2] + b * b
 
-        return [corners(2, g) for g in range(GROUPS)], lines(lax.fori_loop(0, KL, body, zeros[:3]))
-
-    twist_1, sums = exchange(1, totals, known_products)
+        corner_sums(1)
+        return lines(lax.fori_loop(0, KL, body, zeros[:3]))
+
+    lane1 = lax.broadcasted_iota(jnp.int32, (1, HALF), 1)
+
+    def share(stage, row, buffer, count, place):
+        stat[stage] = row
+        for d in range(1, count):
+            remote(stat.at[stage], buffer.at[d - 1], 5 + stage, ar_recv.at[stage], place(d))
+        return row
+
+    def collect(stage, buffer, row):
+        wait_for(buffer, ar_recv.at[stage])
+        return row + jnp.sum(buffer[...], axis=0)
+
+    def start_sum(sums):
+        for n in range(2):
+            wait_for(dbuf.at[n], d_recv.at[n])
+        crossed = [jnp.zeros((8, HALF), F32)] * 2
+        lane8 = lax.broadcasted_iota(jnp.int32, (8, HALF), 1)
+        for piece in range(pieces):
+            mine = rows_of(m * pieces + piece)
+            value = [wrows[h, mine, :] * agbuf[1, h, mine, :] for h in range(2)]
+            outer = jnp.where(lane8 < 8, value[0], jnp.where(lane8 >= 120, value[1], 0.0))
+            for n in range(2):
+                corner = dinc[n, mine, :]
+                for d in range(1, mems):
+                    corner = corner + dbuf[n, d - 1, piece]
+                crossed[n] = crossed[n] + (
+                    agbuf[n, 0, mine, :] * value[0] + agbuf[n, 1, mine, :] * value[1] + corner * outer
+                )
+        row = jnp.zeros((1, HALF), F32)
+        for i, line in enumerate(sums + [jnp.sum(total, axis=0, keepdims=True) for total in crossed]):
+            row = jnp.where(lane1 == i, jnp.sum(line, axis=1, keepdims=True), row)
+        return share(0, row, ar2, depth, at_depth)
+
+    shared = exchange(1, totals, known_products, start_sum)
     values = weighted(1)
     for g in range(GROUPS):
         adjoint(g, values, g1)
-        send_edges(3, g, g1)
+        pack_edges(3, g, g1)
+        send_edges(3, g)
         send_rows(3, g, g1)
-
-    def new_products(k, totals):
-        return totals[0] + u0[k] * g1[k], totals[1] + u1[k] * g1[k]
-
-    totals = lax.fori_loop(0, KL, new_products, zeros[:2])
-    totals = [
-        total + sum(twist[g] * packs[3, g] for g in range(GROUPS)) for total, twist in zip(totals, (twist_0, twist_1))
-    ]
-    sums = sums + lines(totals)
-    lane1 = lax.broadcasted_iota(jnp.int32, (1, HALF), 1)
-    row = jnp.zeros((1, HALF), F32)
-    for i, line in enumerate(sums):
-        row = jnp.where(lane1 == i, jnp.sum(line, axis=1, keepdims=True), row)
-
-    def share(stage, buffer, count, place, base):
-        stat[stage] = row
-        return [
-            remote(stat.at[stage], buffer.at[d - 1], ar_send.at[base + d], ar_recv.at[base + d], place(d))
-            for d in range(1, count)
-        ]
-
-    def collect(buffer, waited):
-        for copy in waited:
-            copy.wait_recv()
-        return row + jnp.sum(buffer[...], axis=0)
-
-    shared = share(0, ar1, 4 * mems, at_plane, 0)
-    for g in range(GROUPS - 1):
+    shared = share(1, collect(0, ar2, shared), ar1, 4 * mems, at_plane)
+    for g in range(GROUPS):
         smooth(3, g, g1, v2)
-    row = collect(ar1, shared)
-    shared = share(1, ar2, depth, at_depth, 4 * mems)
-    smooth(3, GROUPS - 1, g1, v2)
-    row = collect(ar2, shared)
+    row = collect(1, ar1, shared)
 
     aa, ab, bb, ac, bc = (
         jnp.sum(jnp.where(lane1 == i, row, 0.0), axis=1, keepdims=True) for i in range(5)
@@ -367,8 +389,8 @@
         a, b, c = v0[k], v1[k], v2[k]
         w_out[0, k] = w0 * a + w1 * b
         r_out[0, k] = q0 * a + q1 * b + q2 * c
-    for copy in sends:
-        copy.wait_send()
+    for kind, buffer in enumerate((rhalo, ehalo, rsbuf, rsbuf, dbuf, ar2, ar1)):
+        wait_for(buffer, send_sem.at[kind])
 
 
 def local(tiles, tcols, mems, right_side, perturbations, precision, covered):
@@ -385,27 +407,28 @@
         pltpu.VMEM((32, TX), f32),
         pltpu.VMEM((32, TX), f32),
         pltpu.VMEM((6, KL, TY, TX), f32),
-        pltpu.VMEM((4, GROUPS, KG, 8, TX), f32),
-        pltpu.VMEM((4, GROUPS, KG, 8, TX), f32),
+        pltpu.VMEM((4, GROUPS, 2, KG, 8, TX), f32),
         pltpu.VMEM((4, GROUPS, 32, TX), f32),
         pltpu.VMEM((4, GROUPS, TY, TX), f32),
         pltpu.VMEM((2, 2, 128, HALF), f32),
         pltpu.VMEM((2, mems - 1, pieces, 2, 8, HALF), f32),
         pltpu.VMEM((2, 2, 128, HALF), f32),
+        pltpu.VMEM((2, 128, HALF), f32),
+        pltpu.VMEM((2, 128, HALF), f32),
+        pltpu.VMEM((2, mems - 1, pieces, 8, HALF), f32),
         pltpu.VMEM((2, 1, HALF), f32),
         pltpu.VMEM((4 * mems - 1, 1, HALF), f32),
         pltpu.VMEM((tiles // 4 - 1, 1, HALF), f32),
         pltpu.SemaphoreType.DMA((9,)),
-        pltpu.SemaphoreType.DMA((4, GROUPS, 8)),
-        pltpu.SemaphoreType.DMA((4, GROUPS, 8)),
-        pltpu.SemaphoreType.DMA((2, mems - 1, pieces)),
-        pltpu.SemaphoreType.DMA((2, mems - 1, pieces)),
-        pltpu.SemaphoreType.DMA((2, mems - 1, pieces)),
-        pltpu.SemaphoreType.DMA((2, mems - 1, pieces)),
-        pltpu.SemaphoreType.DMA((4 * mems + tiles // 4,)),
-        pltpu.SemaphoreType.DMA((4 * mems + tiles // 4,)),
+        pltpu.SemaphoreType.DMA((7,)),
+        pltpu.SemaphoreType.DMA((4, GROUPS)),
+        pltpu.SemaphoreType.DMA((4, GROUPS)),
+        pltpu.SemaphoreType.DMA((2,)),
+        pltpu.SemaphoreType.DMA((2,)),
+        pltpu.SemaphoreType.DMA((2,)),
+        pltpu.SemaphoreType.DMA((2,)),
     ]
-    return pl.pallas_call(
+    results = pl.pallas_call(
         functools.partial(kernel, tiles, tcols, mems),
         out_shape=(field, field),
         in_specs=[pl.BlockSpec(memory_space=pltpu.MemorySpace.HBM)] * 9,
@@ -416,6 +439,23 @@
         ),
         name="conjugate_gradients",
     )(*[pltpu.with_memory_space_constraint(x, pltpu.MemorySpace.HBM) for x in (right_side, perturbations, precision, covered, *constants)])
+    return pl.pallas_call(
+        put_out,
+        out_shape=(field, field),
+        in_specs=[pl.BlockSpec(memory_space=pltpu.MemorySpace.VMEM)] * 2,
+        out_specs=(pl.BlockSpec(memory_space=pltpu.MemorySpace.HBM),) * 2,
+        scratch_shapes=[pltpu.SemaphoreType.DMA((2,))],
+        compiler_params=pltpu.CompilerParams(vmem_limit_bytes=2**20),
+        name="put_out",
+    )(*results)
+
+
+def put_out(w_in, r_in, w_out, r_out, sem):
+    copies = [pltpu.make_async_copy(a, b, sem.at[i]) for i, (a, b) in enumerate(((w_in, w_out), (r_in, r_out)))]
+    for copy in copies:
+        copy.start()
+    for copy in copies:
+        copy.wait()
 
 
 def solution(mesh, tcols=8):

time: 93.4 us -> 85.1 us (0.911)
  Pallas kernels: 91.2 us -> 84.3 us
  local copies, waits for them, and re-layouts: 1.41 us -> 0 us
    pallas_call x1, Pallas kernels: 91.2 us -> 83.5 us  [local(): pl.pallas_call(functools.partial(kernel, tiles, tcols, mems), out_shape=(...]
    unnamed x2 -> x0, local copies, waits for them, and re-layouts: 1.41 us -> none
where the time goes in v3:
time: 85.1 us; the launch traced here: 84.9 us
  Pallas kernels  84.3 us (99%)
    pallas_call x1, Pallas kernels, local(): pl.pallas_call(functools.partial(kernel, tiles, tcols, mems), out_shape=(...  83.5 us

profile of v3, /device:TPU:2, one launch (start us, length us, event | category | flops | bytes accessed | tf_op | source)
XLA Modules:
  0.0 84.9 jit_solution(8595360725358444602)
XLA Ops:
  0.6 83.5 %conjugate_gradients.1 = (f32[1,16,16,256]{3,2,1,0:T(8,128)S(1)}, f32[1,16,16,256]{3,2,1,0:T(8,128)S(1)}) custom-call(f32[1,16,16,256]{3,2,1,0:T(8,128)} %src_hbm.1, bf16[1,16,6,16,256]{4,3,2,1,0:T(8,128)(2,1)} %pert_hbm.1, f32[1,6,16,256]{3,2,1,0:T(8,128)} %prec_hbm.1, s32[1,2,16]{2,1,0:T(2,128)} %cov_hbm.1, bf16[128,768]{1,0:T(8,128)(2,1)} %constant.10.clone.rows_hbm, ...), custom_call_target="tpu_custom_call" | custom-call | tf_op jit(solution)/shard_map/conjugate_gradients/pallas_call | solution.py:431
  84.1 0.8 put_out.1

commit v4 on v3

--- a/solution.py
+++ b/solution.py
@@ -192,7 +192,7 @@
     pieces = TY // mems
 
     def rows_of(y):
-        return pl.ds(pl.multiple_of(8 * y, 8), 8)
+        return pl.ds(pl.multiple_of(8 * y, 8), VL)
 
     def send_corners(n, twist):
         def body(i, totals):
@@ -344,8 +344,8 @@
     def start_sum(sums):
         for n in range(2):
             wait_for(dbuf.at[n], d_recv.at[n])
-        crossed = [jnp.zeros((8, HALF), F32)] * 2
-        lane8 = lax.broadcasted_iota(jnp.int32, (8, HALF), 1)
+        crossed = [jnp.zeros((VL, HALF), F32)] * 2
+        lane8 = lax.broadcasted_iota(jnp.int32, (VL, HALF), 1)
         for piece in range(pieces):
             mine = rows_of(m * pieces + piece)
             value = [wrows[h, mine, :] * agbuf[1, h, mine, :] for h in range(2)]
@@ -411,11 +411,11 @@
         pltpu.VMEM((4, GROUPS, 32, TX), f32),
         pltpu.VMEM((4, GROUPS, TY, TX), f32),
         pltpu.VMEM((2, 2, 128, HALF), f32),
-        pltpu.VMEM((2, mems - 1, pieces, 2, 8, HALF), f32),
+        pltpu.VMEM((2, mems - 1, pieces, 2, VL, HALF), f32),
         pltpu.VMEM((2, 2, 128, HALF), f32),
         pltpu.VMEM((2, 128, HALF), f32),
         pltpu.VMEM((2, 128, HALF), f32),
-        pltpu.VMEM((2, mems - 1, pieces, 8, HALF), f32),
+        pltpu.VMEM((2, mems - 1, pieces, VL, HALF), f32),
         pltpu.VMEM((2, 1, HALF), f32),
         pltpu.VMEM((4 * mems - 1, 1, HALF), f32),
         pltpu.VMEM((tiles // 4 - 1, 1, HALF), f32),

time: 85.1 us -> 83.6 us (0.982)
  the two profiles are of different devices: /device:TPU:2 before, /device:TPU:16 now
where the time goes in v4:
time: 83.6 us; the launch traced here: 83.5 us
  Pallas kernels  82.8 us (99%)
    pallas_call x1, Pallas kernels, local(): pl.pallas_call(functools.partial(kernel, tiles, tcols, mems), out_shape=(...  82 us

profile of v4, /device:TPU:16, one launch (start us, length us, event | category | flops | bytes accessed | tf_op | source)
XLA Modules:
  0.0 83.5 jit_solution(14438169141373425451)
XLA Ops:
  0.6 82.0 %conjugate_gradients.1 = (f32[1,16,16,256]{3,2,1,0:T(8,128)S(1)}, f32[1,16,16,256]{3,2,1,0:T(8,128)S(1)}) custom-call(f32[1,16,16,256]{3,2,1,0:T(8,128)} %src_hbm.1, bf16[1,16,6,16,256]{4,3,2,1,0:T(8,128)(2,1)} %pert_hbm.1, f32[1,6,16,256]{3,2,1,0:T(8,128)} %prec_hbm.1, s32[1,2,16]{2,1,0:T(2,128)} %cov_hbm.1, bf16[128,768]{1,0:T(8,128)(2,1)} %constant.10.clone.rows_hbm, ...), custom_call_target="tpu_custom_call" | custom-call | tf_op jit(solution)/shard_map/conjugate_gradients/pallas_call | solution.py:431
  82.6 0.8 put_out.1
